TPU v7x, 128 devices: a whole 4x4x4 slice. The times are simulated.
128 devices in a mesh: dp: 16 (over z, x), tensor: 8 (over y, core).
Axes of the slice: x: 4, y: 4, z: 4, core: 2. Of those that a mesh axis runs over, the one named last changes fastest.
Arguments:
- inputs: bfloat16 [6144, 12288], P('dp', 'tensor'), may hold values from -160 to 160
- out_grad: bfloat16 [6144, 6144], P('dp'), may hold values from -0.08930431 to 0.08930431
- weight_codes: bfloat16 [6144, 12288], P('dp', 'tensor'), may hold values from -1 to 1
- weight_scales: bfloat16 [6144], P('dp'), may hold values from 0.0039978027 to 0.019897461
- master: float32 [6144, 12288], P('dp', 'tensor'), may hold values from -0.8 to 0.8
- moment: float32 [6144, 12288], P('dp', 'tensor'), may hold values from -3 to 3
- second: float32 [6144, 12288], P('dp', 'tensor'), may hold values from 0.05 to 0.5
Outputs:
- grad_input: bfloat16 [6144, 12288], P('dp', 'tensor')
- new_master: float32 [6144, 12288], P('dp', 'tensor')
- new_moment: float32 [6144, 12288], P('dp', 'tensor')
- new_second: float32 [6144, 12288], P('dp', 'tensor')
- new_codes: bfloat16 [6144, 12288], P('dp', 'tensor')
- new_scales: bfloat16 [6144], P('dp')
- grad_peak: float32 [], replicated
All inputs are finite; a program needn't handle non-finite values. Where the computation divides by a largest or mean magnitude, that divisor is 1e-20 or more.
Results may differ from a plain program's by a relative error of at most 0.019.
Values may be sent and summed in bfloat16 or wider, within the bound.
No kernel may reach another device: no remote copies, remote signals or barrier semaphores. Data moves between devices by JAX's collectives and lax.ppermute only.
A program may use at most 192 MiB of HBM per device.

v0:
```python
import functools
import jax
import jax.numpy as jnp
from jax import lax
from jax.experimental import pallas as pl
from jax.experimental.pallas import tpu as pltpu
from jax.sharding import Mesh
from jax.sharding import PartitionSpec as P

ALL = ("z", "x", "y", "c")
DP = ("z", "x")
TENSOR = ("y", "c")
IN = 12288
OUT = 6144
S = 384
C = 1536
HALF = S // 2
SUB = S // 8
NT = 256
BF = jnp.bfloat16
F32 = jnp.float32
RZ = (2, 1, 3, 0)


def shift(v, axis, by):
    n = 4 if axis != "c" else 2
    return lax.ppermute(v, axis, [(i, (i + by) % n) for i in range(n)])


def params(mib):
    return pltpu.CompilerParams(vmem_limit_bytes=mib << 20)


def split_kernel(grad_ref, *refs):
    outs, slab, sem = refs[:3], refs[3], refs[4]
    z, x, y, c = (lax.axis_index(a) for a in ALL)
    top = pl.multiple_of((y * 2 + c) * SUB, SUB)
    copy = pltpu.make_async_copy(grad_ref.at[pl.ds(top, SUB), :], slab, sem)
    copy.start()
    copy.wait()
    for out, rx in zip(outs, (1, 3, 2)):
        for k, rz in enumerate(RZ):
            block = lax.rem(z + rz, 4) * 4 + lax.rem(x + rx, 4)
            out[:, k * S : (k + 1) * S] = slab[:, pl.ds(pl.multiple_of(block * S, S), S)]


def split_grads(out_grad):
    piece = jax.ShapeDtypeStruct((SUB, C), BF)
    return pl.pallas_call(
        split_kernel,
        in_specs=[pl.BlockSpec(memory_space=pltpu.HBM)],
        out_specs=[pl.BlockSpec(memory_space=pltpu.VMEM)] * 3,
        out_shape=[piece] * 3,
        scratch_shapes=[pltpu.VMEM((SUB, OUT), BF), pltpu.SemaphoreType.DMA],
        compiler_params=params(8),
        name="split_grads",
    )(out_grad)


def assemble_kernel(*refs):
    grad_ref, chunks, (rows_ref, cols_ref) = refs[0], refs[1:9], refs[9:]
    z, x, y, c = (lax.axis_index(a) for a in ALL)
    for k, rz in enumerate(RZ):
        block = lax.rem(z + rz, 4) * 4 + x
        rows_ref[0, :, k * S : (k + 1) * S] = grad_ref[:, pl.ds(pl.multiple_of(block * S, S), S)]
    for core in range(2):
        for i, ry in enumerate((0, 3, 1, 2)):
            source = lax.rem(y + ry, 4) * 2 + lax.rem(c + core, 2)
            top = pl.multiple_of(source * SUB, SUB)
            for j in range(3):
                rows_ref[1 + j, pl.ds(top, SUB), :] = chunks[core * 4 + i][
                    j * SUB : (j + 1) * SUB, :
                ]
    for j in range(4):
        for k in range(4):
            cols_ref[k, :, j * S : (j + 1) * S] = rows_ref[j, :, k * S : (k + 1) * S].T


def assemble(out_grad, chunks):
    full = pl.BlockSpec((3 * SUB, C), lambda i: (0, 0))
    out = pl.BlockSpec((4, S, C), lambda i: (0, 0, 0))
    return pl.pallas_call(
        assemble_kernel,
        grid=(1,),
        in_specs=[pl.BlockSpec((S, OUT), lambda i: (0, 0))] + [full] * 8,
        out_specs=[out, out],
        out_shape=[jax.ShapeDtypeStruct((4, S, C), BF)] * 2,
        compiler_params=params(28),
        name="assemble_grads",
    )(out_grad, *chunks)


def weight_grad_kernel(blocks, width, *refs):
    count = len(blocks)
    cols, acts, outs = refs[:count], refs[count : count + 5], refs[count + 5 :]
    peak_ref = outs[-1]
    peak_ref[...] = jnp.zeros_like(peak_ref)

    def step(i, carry):
        at = pl.ds(pl.multiple_of(i * NT, NT), NT)
        right = [acts[j][:, at] for j in range(3)]
        right.append(jnp.concatenate([acts[3][:, at], acts[4][:, at]], axis=0))
        peak = peak_ref[...]
        n = 0
        for k, block in enumerate(blocks):
            total = None
            for j in range(4):
                part = jnp.dot(
                    cols[k][0, :, j * S : (j + 1) * S], right[j], preferred_element_type=F32
                )
                high = jnp.max(jnp.abs(part).reshape(S // 8, 8, NT), axis=0)
                peak = jnp.maximum(peak, high)
                total = part if total is None else total + part
            if block == 3:
                outs[n][:, at] = total
                n += 1
            else:
                outs[n][:, at] = total[:HALF].astype(BF)
                outs[n + 1][:, at] = total[HALF:].astype(BF)
                n += 2
        peak_ref[...] = peak
        return carry

    lax.fori_loop(0, width // NT, step, 0)


def weight_grad(cols, blocks, acts):
    width = acts[0].shape[1]
    outs = []
    for block in blocks:
        if block == 3:
            outs.append(jax.ShapeDtypeStruct((S, width), F32))
        else:
            outs += [jax.ShapeDtypeStruct((HALF, width), BF)] * 2
    outs.append(jax.ShapeDtypeStruct((8, NT), F32))

    def piece(k):
        return pl.BlockSpec((1, S, C), lambda i: (k, 0, 0))

    def whole(v):
        return pl.BlockSpec(v.shape, lambda i: (0, 0))

    return pl.pallas_call(
        functools.partial(weight_grad_kernel, blocks, width),
        grid=(1,),
        in_specs=[piece(k) for k in blocks] + [whole(v) for v in acts],
        out_specs=[whole(v) for v in outs],
        out_shape=outs,
        compiler_params=params(24),
        cost_estimate=pl.CostEstimate(
            flops=2 * len(blocks) * S * C * width, bytes_accessed=9 << 20, transcendentals=0
        ),
        name="weight_grad",
    )(*([cols] * len(blocks)), *acts)


def far_start_kernel(cols_ref, own_ref, left_ref, right_ref, part_ref, peak_ref):
    peak_ref[...] = jnp.zeros_like(peak_ref)

    def step(i, carry):
        at = pl.ds(pl.multiple_of(i * NT, NT), NT)
        peak, total = peak_ref[...], None
        for j, ref in enumerate((own_ref, left_ref, right_ref)):
            part = jnp.dot(
                cols_ref[0, :, j * S : (j + 1) * S], ref[:, at], preferred_element_type=F32
            )
            peak = jnp.maximum(peak, jnp.max(jnp.abs(part).reshape(S // 8, 8, NT), axis=0))
            total = part if total is None else total + part
        part_ref[:, at] = total
        peak_ref[...] = peak
        return carry

    lax.fori_loop(0, C // NT, step, 0)


def far_finish_kernel(cols_ref, part_ref, top_ref, low_ref, peak_in, high_ref, low_out, peak_ref):
    peak_ref[...] = peak_in[...]

    def step(i, carry):
        at = pl.ds(pl.multiple_of(i * NT, NT), NT)
        right = jnp.concatenate([top_ref[:, at], low_ref[:, at]], axis=0)
        part = jnp.dot(cols_ref[0], right, preferred_element_type=F32)
        high = jnp.max(jnp.abs(part).reshape(S // 8, 8, NT), axis=0)
        peak_ref[...] = jnp.maximum(peak_ref[...], high)
        total = part_ref[:, at] + part
        high_ref[:, at] = total[:HALF].astype(BF)
        low_out[:, at] = total[HALF:].astype(BF)
        return carry

    lax.fori_loop(0, C // NT, step, 0)


def whole(shape):
    return pl.BlockSpec(shape, lambda i: (0,) * len(shape))


def weight_grad_far(cols, acts):
    small = jax.ShapeDtypeStruct((8, NT), F32)
    half = jax.ShapeDtypeStruct((HALF, C), BF)
    part, peak = pl.pallas_call(
        far_start_kernel,
        grid=(1,),
        in_specs=[whole((1, S, C))] + [whole((S, C))] * 3,
        out_specs=[whole((S, C)), whole((8, NT))],
        out_shape=[jax.ShapeDtypeStruct((S, C), F32), small],
        compiler_params=params(24),
        cost_estimate=pl.CostEstimate(
            flops=6 * S * S * C, bytes_accessed=6 << 20, transcendentals=0
        ),
        name="far_start",
    )(cols, *acts[:3])
    return pl.pallas_call(
        far_finish_kernel,
        grid=(1,),
        in_specs=[
            pl.BlockSpec((1, S, S), lambda i: (0, 0, 3)),
            whole((S, C)),
            whole((HALF, C)),
            whole((HALF, C)),
            whole((8, NT)),
        ],
        out_specs=[whole((HALF, C)), whole((HALF, C)), whole((8, NT))],
        out_shape=[half, half, small],
        compiler_params=params(24),
        cost_estimate=pl.CostEstimate(
            flops=2 * S * S * C, bytes_accessed=4 << 20, transcendentals=0
        ),
        name="far_finish",
    )(cols, part, acts[3], acts[4], peak)


STEP = 32


def fold_kernel(chunks, *refs):
    grad_ref, pair_ref = refs[-2:]
    peaks = refs[5 * len(chunks) : -2]

    squares = jnp.zeros((8, 128), F32)
    for k, (low, width) in enumerate(chunks):
        own, top_l, low_l, top_r, low_r = refs[5 * k : 5 * k + 5]

        def step(i, total, own=own, low=low, width=width, arms=((0, top_l, top_r), (HALF, low_l, low_r))):
            at = pl.multiple_of(i * STEP, STEP)
            for base, left, right in arms:
                rows = pl.ds(at, STEP)
                value = (
                    own[pl.ds(base + at, STEP), :]
                    + left[rows, :].astype(F32)
                    + right[rows, :].astype(F32)
                )
                grad_ref[pl.ds(base + at, STEP), low : low + width] = value
                square = (value * value).reshape(STEP // 8, 8, width).sum(axis=0)
                for j in range(width // 128):
                    total = total + square[:, j * 128 : (j + 1) * 128]
            return total

        squares = lax.fori_loop(0, HALF // STEP, step, squares)
    peak = peaks[0][...]
    for ref in peaks[1:]:
        peak = jnp.maximum(peak, ref[...])
    lane = lax.broadcasted_iota(jnp.int32, (128, 128), 1)
    pair_ref[...] = jnp.where(lane < 64, jnp.sum(squares), jnp.max(peak))


def fold_grad(parts, chunks, peaks):
    args = [v for part in parts for v in part] + list(peaks)
    return pl.pallas_call(
        functools.partial(fold_kernel, chunks),
        grid=(1,),
        in_specs=[pl.BlockSpec(v.shape, lambda i: (0, 0)) for v in args],
        out_specs=[
            pl.BlockSpec((S, C), lambda i: (0, 0)),
            pl.BlockSpec((128, 128), lambda i: (0, 0)),
        ],
        out_shape=[pltpu.HBM((S, C), F32), jax.ShapeDtypeStruct((128, 128), F32)],
        compiler_params=params(24),
        name="fold_grad",
    )(*args)


ROWS = 96


def adam_kernel(
    pairs_ref, grad_ref, moment_ref, second_ref, master_ref,
    moment_out, second_out, master_out, high_out, peak_out, again_ref, high_ref,
):
    i = pl.program_id(0)
    pairs = pairs_ref[...]
    squares = jnp.sum(pairs, axis=0, keepdims=True)[:, :1]
    clip_factor = jnp.minimum(1.0, jnp.sqrt(F32(OUT * IN)) / (jnp.sqrt(squares) + 1e-06))
    clipped = clip_factor * grad_ref[...]
    new_moment = 0.9 * moment_ref[...] + 0.1 * clipped
    new_second = 0.95 * second_ref[...] + 0.05 * clipped * clipped
    master = master_ref[...]
    new_master = master - 0.01 * (new_moment / (jnp.sqrt(new_second) + 1e-08) + 0.1 * master)
    moment_out[...] = new_moment
    second_out[...] = new_second
    master_out[...] = new_master
    again_ref[...] = new_master
    size = jnp.abs(new_master)
    high = size[:, :128]
    for j in range(1, C // 128):
        high = jnp.maximum(high, size[:, j * 128 : (j + 1) * 128])
    high_ref[pl.ds(pl.multiple_of(i * ROWS, ROWS), ROWS), :] = high

    @pl.when(i == S // ROWS - 1)
    def _():
        highs = jnp.max(high_ref[...].T, axis=0, keepdims=True)
        high_out[...] = jnp.broadcast_to(highs.reshape(1, 1, S), (8, 1, S))
        peak_out[...] = jnp.broadcast_to(jnp.max(pairs, axis=0, keepdims=True), (8, 128))


def adam(pairs, gradient, moment, second, master):
    block = pl.BlockSpec((ROWS, C), lambda i: (i, 0))
    small = jax.ShapeDtypeStruct((8, 128), F32)
    return pl.pallas_call(
        adam_kernel,
        grid=(S // ROWS,),
        in_specs=[pl.BlockSpec((128, 128), lambda i: (0, 0))] + [block] * 4,
        out_specs=[block] * 3
        + [whole((8, 1, S)), whole((8, 128)), block],
        out_shape=[jax.ShapeDtypeStruct((S, C), F32)] * 3
        + [jax.ShapeDtypeStruct((8, 1, S), F32), small, pltpu.VMEM((S, C), F32)],
        scratch_shapes=[pltpu.VMEM((S, 128), F32)],
        compiler_params=params(16),
        name="adam",
    )(pairs, gradient, moment, second, master)


def input_grad_kernel(count, own_last, *refs):
    rows, weights, outs = refs[:count], refs[count : count + 5], refs[count + 5 :]

    def step(i, carry):
        at = pl.ds(pl.multiple_of(i * NT, NT), NT)
        right = jnp.concatenate([w[:, at] for w in weights], axis=0)
        for k in range(count):
            total = jnp.dot(rows[k][0], right, preferred_element_type=F32)
            if own_last:
                outs[k][:, at] = total
            else:
                outs[2 * k][:, at] = total[:HALF].astype(BF)
                outs[2 * k + 1][:, at] = total[HALF:].astype(BF)
        return carry

    lax.fori_loop(0, C // NT, step, 0)


def input_grad(rows, blocks, weights, own):
    half = jax.ShapeDtypeStruct((HALF, C), BF)
    outs = [jax.ShapeDtypeStruct((S, C), F32)] if own else [half] * (2 * len(blocks))

    def piece(k):
        return pl.BlockSpec((1, S, C), lambda i: (k, 0, 0))

    def whole(v):
        return pl.BlockSpec(v.shape, lambda i: (0, 0))

    return pl.pallas_call(
        functools.partial(input_grad_kernel, len(blocks), own),
        grid=(1,),
        in_specs=[piece(k) for k in blocks] + [whole(v) for v in weights],
        out_specs=[whole(v) for v in outs],
        out_shape=outs,
        compiler_params=params(24),
        cost_estimate=pl.CostEstimate(
            flops=2 * len(blocks) * S * C * C, bytes_accessed=9 << 20, transcendentals=0
        ),
        name="input_grad",
    )(*([rows] * len(blocks)), *weights)


def codes_kernel(highs_ref, master_ref, codes_ref, scales_ref):
    row_peak = jnp.max(highs_ref[...], axis=0) + 1e-06
    scales_ref[...] = row_peak
    column = jnp.broadcast_to(row_peak, (128, S)).T
    for j in range(C // 128):
        at = slice(j * 128, (j + 1) * 128)
        codes_ref[:, at] = (master_ref[:, at] / column).astype(BF)


def codes(highs, master):
    return pl.pallas_call(
        codes_kernel,
        grid=(1,),
        in_specs=[whole((8, 1, S)), whole((S, C))],
        out_specs=[whole((S, C)), whole((1, S))],
        out_shape=[jax.ShapeDtypeStruct((S, C), BF), jax.ShapeDtypeStruct((1, S), F32)],
        compiler_params=params(16),
        name="codes",
    )(highs, master)


def ring_gather(v, axis):
    left = shift(v, axis, 1)
    right = shift(v, axis, -1)
    top = shift(left[:HALF], axis, 1)
    bottom = shift(right[HALF:], axis, -1)
    return v, left, right, top, bottom


def ring_scatter(far, near, axis):
    up_a, up_b, down_a, down_b = near
    from_left = shift(far[0], axis, 1)
    from_right = shift(far[1], axis, -1)
    left_b = shift(up_b, axis, 1)
    right_a = shift(down_a, axis, -1)
    up_a = (up_a.astype(F32) + from_left.astype(F32)).astype(BF)
    down_b = (down_b.astype(F32) + from_right.astype(F32)).astype(BF)
    left_a = shift(up_a, axis, 1)
    right_b = shift(down_b, axis, -1)
    return left_a, left_b, right_a, right_b


CHUNKS = ((0, C),)


def step(inputs, out_grad, weight_codes, weight_scales, master, moment, second):
    to_up, to_down, to_far = split_grads(
        pltpu.with_memory_space_constraint(out_grad, pltpu.HBM)
    )
    mine = [shift(to_up, "x", 1), shift(to_down, "x", -1), shift(to_far, "x", 2)]
    mine = jnp.concatenate(mine, axis=0)
    acts = [ring_gather(inputs[:, low : low + width], "x") for low, width in CHUNKS]
    held = [mine] + [shift(mine, "y", s) for s in (1, -1, 2)]
    other = [shift(v, "c", 1) for v in held]
    rows, cols = assemble(out_grad, held + other)

    weight = (weight_codes.astype(F32) * weight_scales.astype(F32)[:, None]).astype(BF)
    ring = ring_gather(weight, "z")
    weights = (*ring[3:], ring[2], ring[1], ring[0])

    parts, peaks = [], []
    for act in acts:
        far_a, far_b, peak_a = weight_grad_far(cols, act)
        *near, own, peak_b = weight_grad(cols, (1, 2, 3), act)
        peaks += [peak_a, peak_b]
        parts.append((own, *ring_scatter((far_a, far_b), near, "z")))

    rows, _ = lax.optimization_barrier((rows, own))
    i_far = input_grad(rows, (3,), weights, False)
    i_near = input_grad(rows, (2, 1), weights, False)
    (i_own,) = input_grad(rows, (0,), weights, True)
    left_a, left_b, right_a, right_b = ring_scatter(i_far, i_near, "x")
    top = i_own[:HALF] + left_a.astype(F32) + right_a.astype(F32)
    bottom = i_own[HALF:] + left_b.astype(F32) + right_b.astype(F32)
    grad_input = jnp.concatenate([top, bottom], axis=0).astype(BF)

    gradient, pair = fold_grad(parts, CHUNKS, peaks)
    pairs = lax.all_to_all(pair, ALL, 0, 0, tiled=True)
    gradient, moment, second, master = (
        pltpu.with_memory_space_constraint(v, pltpu.HBM)
        for v in (gradient, moment, second, master)
    )
    pairs, grad_input = lax.optimization_barrier((pairs, grad_input))
    new_moment, new_second, new_master, high, peak, again = adam(
        pairs, gradient, moment, second, master
    )
    highs = lax.all_to_all(high, TENSOR, 0, 0, tiled=True)
    new_codes, row_peak = codes(highs, pltpu.with_memory_space_constraint(again, pltpu.VMEM))
    new_scales = row_peak[0].astype(BF)
    return (grad_input, new_master, new_moment, new_second, new_codes, new_scales, peak[0, 64])


def solution(mesh):
    finer = Mesh(mesh.devices.reshape(4, 4, 4, 2), ALL)
    tiled = P(DP, TENSOR)
    in_specs = (tiled, P(DP, None), tiled, P(DP), tiled, tiled, tiled)
    out_specs = (tiled, tiled, tiled, tiled, tiled, P(DP), P())
    return jax.shard_map(step, mesh=finer, in_specs=in_specs, out_specs=out_specs, check_vma=False)
```

profile of v0, /device:TPU:1, one launch (start us, length us, event | category | flops | bytes accessed | tf_op | source)
XLA Modules:
  0.0 185.8 jit_solution(17247082947553536323)
XLA Ops:
  2.0 2.1 %collective-permute-start = (bf16[48,1536]{1,0:T(8,128)(2,1)S(1)}, bf16[48,1536]{1,0:T(8,128)(2,1)S(1)}, u32[]{:S(2)}, u32[]{:S(2)}) collective-permute-start(bf16[48,1536]{1,0:T(8,128)(2,1)S(1)} %get-tuple-element.42), channel_id=1, source_target_pairs={{0,8},{8,16},{16,24},{24,0},{1,9},{9,17},{17,25},{25,1},{2,10},{10... | collective-permute-start | bytes 442376 | tf_op jit(solution)/shard_map/ppermute | solution.py:27
  6.9 1.6 collective-permute-start.2
  8.6 26.2 %collective-permute-done.1 = bf16[48,1536]{1,0:T(8,128)(2,1)S(1)} collective-permute-done((bf16[48,1536]{1,0:T(8,128)(2,1)S(1)}, bf16[48,1536]{1,0:T(8,128)(2,1)S(1)}, u32[]{:S(2)}, u32[]{:S(2)}) %collective-permute-start.1) | collective-permute-done | bytes 147488 | tf_op jit(solution)/shard_map/ppermute | solution.py:27
  34.7 3.5 %collective-permute-done.2 = bf16[48,1536]{1,0:T(8,128)(2,1)S(1)} collective-permute-done((bf16[48,1536]{1,0:T(8,128)(2,1)S(1)}, bf16[48,1536]{1,0:T(8,128)(2,1)S(1)}, u32[]{:S(2)}, u32[]{:S(2)}) %collective-permute-start.2) | collective-permute-done | bytes 147488 | tf_op jit(solution)/shard_map/ppermute | solution.py:27
  42.9 6.9 %collective-permute-done.3.refs_2_ = bf16[144,1536]{1,0:T(8,128)(2,1)S(1)} collective-permute-done((bf16[144,1536]{1,0:T(8,128)(2,1)S(1)}, bf16[144,1536]{1,0:T(8,128)(2,1)S(1)}, u32[]{:S(2)}, u32[]{:S(2)}) %collective-permute-start.3) | collective-permute-done | bytes 442400 | tf_op jit(solution)/shard_map/ppermute | solution.py:27
  49.8 1.6 collective-permute-start.20
  51.5 2.1 %collective-permute-start.22 = (bf16[384,1536]{1,0:T(8,128)(2,1)S(1)}, bf16[384,1536]{1,0:T(8,128)(2,1)S(1)}, u32[]{:S(2)}, u32[]{:S(2)}) collective-permute-start(bf16[384,1536]{1,0:T(8,128)(2,1)S(1)} %multiply_convert_fusion.refs_5_.refs_6_), channel_id=1, source_target_pairs={{0,96},{32,0},{64,32},{96,64},{1,97},{33,1},{65,33},{97,65},{2,98}... | collective-permute-start | bytes 3538952 | tf_op jit(solution)/shard_map/ppermute | solution.py:27
  53.6 6.8 %collective-permute-done.5.refs_4_ = bf16[144,1536]{1,0:T(8,128)(2,1)S(1)} collective-permute-done((bf16[144,1536]{1,0:T(8,128)(2,1)S(1)}, bf16[144,1536]{1,0:T(8,128)(2,1)S(1)}, u32[]{:S(2)}, u32[]{:S(2)}) %collective-permute-start.5) | collective-permute-done | bytes 442400 | tf_op jit(solution)/shard_map/ppermute | solution.py:27
  60.4 4.6 %collective-permute-start.6 = (bf16[144,1536]{1,0:T(8,128)(2,1)S(1)}, bf16[144,1536]{1,0:T(8,128)(2,1)S(1)}, u32[]{:S(2)}, u32[]{:S(2)}) collective-permute-start(bf16[144,1536]{1,0:T(8,128)(2,1)S(1)} %constant_dynamic-update-slice_fusion.refs_1_), channel_id=1, source_target_pairs={{0,1},{1,0},{2,3},{3,2},{4,5},{5,4},{6,7},{7,6},{8,9},{9,8},{10,11... | collective-permute-start | bytes 1327112 | tf_op jit(solution)/shard_map/ppermute | solution.py:27
  67.1 2.0 %collective-permute-start.13 = (bf16[192,1536]{1,0:T(8,128)(2,1)S(1)}, bf16[192,1536]{1,0:T(8,128)(2,1)S(1)}, u32[]{:S(2)}, u32[]{:S(2)}) collective-permute-start(bf16[192,1536]{1,0:T(8,128)(2,1)S(1)} %slice.29), channel_id=1, source_target_pairs={{0,24},{8,0},{16,8},{24,16},{1,25},{9,1},{17,9},{25,17},{2,26},{10... | collective-permute-start | bytes 1769480 | tf_op jit(solution)/shard_map/ppermute | solution.py:27
  71.5 1.6 assemble_grads.1
  73.1 3.7 %collective-permute-done.20.refs_4_.refs_5_ = bf16[384,1536]{1,0:T(8,128)(2,1)S(1)} collective-permute-done((bf16[384,1536]{1,0:T(8,128)(2,1)S(1)}, bf16[384,1536]{1,0:T(8,128)(2,1)S(1)}, u32[]{:S(2)}, u32[]{:S(2)}) %collective-permute-start.20) | collective-permute-done | bytes 1179680 | tf_op jit(solution)/shard_map/ppermute | solution.py:27
  77.0 2.7 %collective-permute-start.23 = (bf16[192,1536]{1,0:T(8,128)(2,1)S(1)}, bf16[192,1536]{1,0:T(8,128)(2,1)S(1)}, u32[]{:S(2)}, u32[]{:S(2)}) collective-permute-start(bf16[192,1536]{1,0:T(8,128)(2,1)S(1)} %slice.31), channel_id=1, source_target_pairs={{0,96},{32,0},{64,32},{96,64},{1,97},{33,1},{65,33},{97,65},{2,98}... | collective-permute-start | bytes 1769480 | tf_op jit(solution)/shard_map/ppermute | solution.py:27
  79.7 2.8 %far_start.1 = (f32[384,1536]{1,0:T(8,128)S(1)}, f32[8,256]{1,0:T(8,128)S(1)}) custom-call(bf16[4,384,1536]{2,1,0:T(8,128)(2,1)S(1)} %get-tuple-element.45.refs_0_.refs_1_.refs_2_.cols_ref, bf16[384,1536]{1,0:T(8,128)(2,1)S(1)} %copy-done.1, bf16[384,1536]{1,0:T(8,128)(2,1)S(1)} %collective-permute-done.10.refs_4_.left_ref, ...), custom_call_target="tpu_custom_call" | custom-call | flops 1358954496 | bytes 6291456 | tf_op jit(solution)/shard_map/far_start/pallas_call | solution.py:200
  82.6 1.6 far_finish.1
  84.3 8.4 %weight_grad.1 = (bf16[192,1536]{1,0:T(8,128)(2,1)S(1)}, bf16[192,1536]{1,0:T(8,128)(2,1)S(1)}, bf16[192,1536]{1,0:T(8,128)(2,1)S(1)}, bf16[192,1536]{1,0:T(8,12...) custom-call(bf16[4,384,1536]{2,1,0:T(8,128)(2,1)S(1)} %get-tuple-element.45.refs_0_.refs_1_.refs_2_.cols_ref, ...), custom_call_target="tpu_custom_call" | custom-call | flops 5435817984 | bytes 9437184 | tf_op jit(solution)/shard_map/weight_grad/pallas_call | solution.py:143
  93.4 2.1 %collective-permute-start.17 = (bf16[192,1536]{1,0:T(8,128)(2,1)S(1)}, bf16[192,1536]{1,0:T(8,128)(2,1)S(1)}, u32[]{:S(2)}, u32[]{:S(2)}) collective-permute-start(bf16[192,1536]{1,0:T(8,128)(2,1)S(1)} %get-tuple-element.52), channel_id=1, source_target_pairs={{0,96},{32,0},{64,32},{96,64},{1,97},{33,1},{65,33},{97,65},{2,98}... | collective-permute-start | bytes 1769480 | tf_op jit(solution)/shard_map/ppermute | solution.py:27
  96.9 5.4 %input_grad.4 = (bf16[192,1536]{1,0:T(8,128)(2,1)S(1)}, bf16[192,1536]{1,0:T(8,128)(2,1)S(1)}, bf16[192,1536]{1,0:T(8,128)(2,1)}, bf16[192,1536]{1,0:T(8,128)(2,1)S(1)}) custom-call(bf16[4,384,1536]{2,1,0:T(8,128)(2,1)S(1)} %get-tuple-element.59.refs_0_.refs_1_, bf16[4,384,1536]{2,1,0:T(8,128)(2,1)S(1)} %get-tuple-element.59.refs_0_.refs_1_, ...), custom_call_target="tpu_custom_call" | custom-call | flops 3623878656 | bytes 9437184 | tf_op jit(solution)/shard_map/input_grad/pallas_call | solution.py:360
  102.3 2.0 %collective-permute-start.26 = (bf16[192,1536]{1,0:T(8,128)(2,1)}, bf16[192,1536]{1,0:T(8,128)(2,1)}, u32[]{:S(2)}, u32[]{:S(2)}) collective-permute-start(bf16[192,1536]{1,0:T(8,128)(2,1)} %get-tuple-element.62), channel_id=1, source_target_pairs={{0,24},{8,0},{16,8},{24,16},{1,25},{9,1},{17,9},{25,17},{2,26},{10... | collective-permute-start | bytes 1769480 | tf_op jit(solution)/shard_map/ppermute | solution.py:27
  104.3 2.9 %input_grad.5 = (bf16[192,1536]{1,0:T(8,128)(2,1)S(1)}, bf16[192,1536]{1,0:T(8,128)(2,1)S(1)}) custom-call(bf16[4,384,1536]{2,1,0:T(8,128)(2,1)S(1)} %get-tuple-element.59.refs_0_.refs_1_, bf16[192,1536]{1,0:T(8,128)(2,1)S(1)} %collective-permute-done.21.refs_1_.refs_2_, bf16[192,1536]{1,0:T(8,128)(2,1)S(1)} %collective-permute-done.23.refs_2_.refs_3_, ...), custom_call_target="tpu_custom_call" | custom-call | flops 1811939328 | bytes 9437184 | tf_op jit(solution)/shard_map/input_grad/pallas_call | solution.py:360
  107.5 8.9 %collective-permute-done.18 = bf16[192,1536]{1,0:T(8,128)(2,1)S(1)} collective-permute-done((bf16[192,1536]{1,0:T(8,128)(2,1)S(1)}, bf16[192,1536]{1,0:T(8,128)(2,1)S(1)}, u32[]{:S(2)}, u32[]{:S(2)}) %collective-permute-start.18) | collective-permute-done | bytes 589856 | tf_op jit(solution)/shard_map/ppermute | solution.py:27
  116.3 1.9 %collective-permute-start.28 = (bf16[192,1536]{1,0:T(8,128)(2,1)S(1)}, bf16[192,1536]{1,0:T(8,128)(2,1)S(1)}, u32[]{:S(2)}, u32[]{:S(2)}) collective-permute-start(bf16[192,1536]{1,0:T(8,128)(2,1)S(1)} %get-tuple-element.65), channel_id=1, source_target_pairs={{0,24},{8,0},{16,8},{24,16},{1,25},{9,1},{17,9},{25,17},{2,26},{10... | collective-permute-start | bytes 1769480 | tf_op jit(solution)/shard_map/ppermute | solution.py:27
  120.7 5.0 %collective-permute-done.28 = bf16[192,1536]{1,0:T(8,128)(2,1)S(1)} collective-permute-done((bf16[192,1536]{1,0:T(8,128)(2,1)S(1)}, bf16[192,1536]{1,0:T(8,128)(2,1)S(1)}, u32[]{:S(2)}, u32[]{:S(2)}) %collective-permute-start.28) | collective-permute-done | bytes 589856 | tf_op jit(solution)/shard_map/ppermute | solution.py:27
  125.7 3.4 %collective-permute-start.19 = (bf16[192,1536]{1,0:T(8,128)(2,1)S(1)}, bf16[192,1536]{1,0:T(8,128)(2,1)S(1)}, u32[]{:S(2)}, u32[]{:S(2)}) collective-permute-start(bf16[192,1536]{1,0:T(8,128)(2,1)S(1)} %add_convert_fusion.2), channel_id=1, source_target_pairs={{0,96},{32,0},{64,32},{96,64},{1,97},{33,1},{65,33},{97,65},{2,98}... | collective-permute-start | bytes 1769480 | tf_op jit(solution)/shard_map/ppermute | solution.py:27
  133.1 2.9 %input_grad.3 = f32[384,1536]{1,0:T(8,128)S(1)} custom-call(bf16[4,384,1536]{2,1,0:T(8,128)(2,1)S(1)} %get-tuple-element.59.refs_0_.refs_1_, bf16[192,1536]{1,0:T(8,128)(2,1)S(1)} %collective-permute-done.21.refs_1_.refs_2_, bf16[192,1536]{1,0:T(8,128)(2,1)S(1)} %collective-permute-done.23.refs_2_.refs_3_, ...), custom_call_target="tpu_custom_call" | custom-call | flops 1811939328 | bytes 9437184 | tf_op jit(solution)/shard_map/input_grad/pallas_call | solution.py:360
  136.0 2.0 %fold_grad.1 = (f32[384,1536]{1,0:T(8,128)}, f32[128,128]{1,0:T(8,128)}) custom-call(f32[384,1536]{1,0:T(8,128)S(1)} %get-tuple-element.46.refs_0_, bf16[192,1536]{1,0:T(8,128)(2,1)S(1)} %collective-permute-done.15.refs_1_, bf16[192,1536]{1,0:T(8,128)(2,1)S(1)} %collective-permute-done.16.refs_2_, bf16[192,1536]{1,0:T(8,128)(2,1)S(1)} %collective-permute-done.17.refs_3_, ...), custom_call_target="tpu_custom_call" | custom-call | tf_op jit(solution)/shard_map/fold_grad/pallas_call | solution.py:268
  138.0 19.4 %all-to-all-start = ((f32[128,1,128]{2,1,0:T(1,128)}), f32[128,1,128]{2,1,0:T(1,128)S(1)}, u32[]{:S(2)}, u32[]{:S(2)}) async-start(f32[128,1,128]{2,1,0:T(1,128)} %bitcast.1), calls=%async_computation | async-start | bytes 131072 | tf_op jit(solution)/shard_map/all_to_all | solution.py:451
  157.4 2.1 %fusion.3 = (bf16[192,1536]{1,0:T(8,128)(2,1)S(1)}, bf16[192,1536]{1,0:T(8,128)(2,1)S(1)}) fusion(f32[384,1536]{1,0:T(8,128)S(1)} %input_grad.3, bf16[192,1536]{1,0:T(8,128)(2,1)} %collective-permute-done.26, bf16[192,1536]{1,0:T(8,128)(2,1)} %collective-permute-done.25, bf16[192,1536]{1,0:T(8,128)(2,1)} %collective-permute-done.29, ...), kind=kLoop, calls=%fused_computation.6 | loop fusion | flops 2949120 | bytes 5898240 | tf_op jit(solution)/shard_map/convert
  160.6 6.4 %all-to-all-done = f32[128,1,128]{2,1,0:T(1,128)S(1)} async-done(((f32[128,1,128]{2,1,0:T(1,128)}), f32[128,1,128]{2,1,0:T(1,128)S(1)}, u32[]{:S(2)}, u32[]{:S(2)}) %all-to-all-start) | async-done | bytes 65568 | tf_op jit(solution)/shard_map/all_to_all | solution.py:451
  166.9 8.3 %adam.1 = (f32[384,1536]{1,0:T(8,128)}, f32[384,1536]{1,0:T(8,128)}, f32[384,1536]{1,0:T(8,128)}, f32[8,1,384]{2,1,0:T(1,128)}, f32[8,128]{1,0:T(8,128)S(1)}, /*index=5*/f32[384,1536]{1,0:T(8,128)S(1)}) custom-call(f32[128,128]{1,0:T(8,128)S(1)} %bitcast.5, f32[384,1536]{1,0:T(8,128)} %get-tuple-element.68.grad_ref, f32[384,1536]{1,0:T(8,128)} %moment_ref.1, ...), custom_call_target="tpu_custom_call" | custom-call | tf_op jit(solution)/shard_map/adam/pallas_call | solution.py:318
  175.3 4.0 %all-to-all-start.1 = ((f32[8,1,384]{2,1,0:T(1,128)}), f32[8,1,384]{2,1,0:T(1,128)S(1)}, u32[]{:S(2)}, u32[]{:S(2)}) async-start(f32[8,1,384]{2,1,0:T(1,128)} %get-tuple-element.72), calls=%async_computation.1 | async-start | bytes 24576 | tf_op jit(solution)/shard_map/all_to_all | solution.py:460
  179.9 4.1 %all-to-all-done.1.highs_ref = f32[8,1,384]{2,1,0:T(1,128)S(1)} async-done(((f32[8,1,384]{2,1,0:T(1,128)}), f32[8,1,384]{2,1,0:T(1,128)S(1)}, u32[]{:S(2)}, u32[]{:S(2)}) %all-to-all-start.1) | async-done | bytes 12320 | tf_op jit(solution)/shard_map/all_to_all | solution.py:460
  (68 shorter events, 25.8 us)
Async XLA Ops:
  2.0 6.6 %collective-permute-start = (bf16[48,1536]{1,0:T(8,128)(2,1)S(1)}, bf16[48,1536]{1,0:T(8,128)(2,1)S(1)}, u32[]{:S(2)}, u32[]{:S(2)}) collective-permute-start(bf16[48,1536]{1,0:T(8,128)(2,1)S(1)} %get-tuple-element.42), channel_id=1, source_target_pairs={{0,8},{8,16},{16,24},{24,0},{1,9},{9,17},{17,25},{25,1},{2,10},{10... | collective-permute-start | bytes 442376 | tf_op jit(solution)/shard_map/ppermute | solution.py:27
  4.1 61.0 %collective-permute-start.10 = (bf16[384,1536]{1,0:T(8,128)(2,1)S(1)}, bf16[384,1536]{1,0:T(8,128)(2,1)S(1)}, u32[]{:S(2)}, u32[]{:S(2)}) collective-permute-start(bf16[384,1536]{1,0:T(8,128)(2,1)S(1)} %copy-done.1), channel_id=1, source_target_pairs={{0,8},{8,16},{16,24},{24,0},{1,9},{9,17},{17,25},{25,1},{2,10},{10... | collective-permute-start | bytes 3538952 | tf_op jit(solution)/shard_map/ppermute | solution.py:27
  5.3 59.9 %collective-permute-start.11 = (bf16[384,1536]{1,0:T(8,128)(2,1)S(1)}, bf16[384,1536]{1,0:T(8,128)(2,1)S(1)}, u32[]{:S(2)}, u32[]{:S(2)}) collective-permute-start(bf16[384,1536]{1,0:T(8,128)(2,1)S(1)} %copy-done.1), channel_id=1, source_target_pairs={{0,24},{8,0},{16,8},{24,16},{1,25},{9,1},{17,9},{25,17},{2,26},{10... | collective-permute-start | bytes 3538952 | tf_op jit(solution)/shard_map/ppermute | solution.py:27
  6.7 28.0 %collective-permute-start.1 = (bf16[48,1536]{1,0:T(8,128)(2,1)S(1)}, bf16[48,1536]{1,0:T(8,128)(2,1)S(1)}, u32[]{:S(2)}, u32[]{:S(2)}) collective-permute-start(bf16[48,1536]{1,0:T(8,128)(2,1)S(1)} %get-tuple-element.43), channel_id=1, source_target_pairs={{0,24},{8,0},{16,8},{24,16},{1,25},{9,1},{17,9},{25,17},{2,26},{10... | collective-permute-start | bytes 442376 | tf_op jit(solution)/shard_map/ppermute | solution.py:27
  6.9 31.3 %collective-permute-start.2 = (bf16[48,1536]{1,0:T(8,128)(2,1)S(1)}, bf16[48,1536]{1,0:T(8,128)(2,1)S(1)}, u32[]{:S(2)}, u32[]{:S(2)}) collective-permute-start(bf16[48,1536]{1,0:T(8,128)(2,1)S(1)} %get-tuple-element.44), channel_id=1, source_target_pairs={{0,16},{8,24},{16,0},{24,8},{1,17},{9,25},{17,1},{25,9},{2,18},{10... | collective-permute-start | bytes 442376 | tf_op jit(solution)/shard_map/ppermute | solution.py:27
  38.2 11.6 %collective-permute-start.3 = (bf16[144,1536]{1,0:T(8,128)(2,1)S(1)}, bf16[144,1536]{1,0:T(8,128)(2,1)S(1)}, u32[]{:S(2)}, u32[]{:S(2)}) collective-permute-start(bf16[144,1536]{1,0:T(8,128)(2,1)S(1)} %constant_dynamic-update-slice_fusion.refs_1_), channel_id=1, source_target_pairs={{0,2},{2,4},{4,6},{6,0},{1,3},{3,5},{5,7},{7,1},{8,10},{10,12},{12... | collective-permute-start | bytes 1327112 | tf_op jit(solution)/shard_map/ppermute | solution.py:27
  39.6 11.9 %collective-permute-start.4 = (bf16[144,1536]{1,0:T(8,128)(2,1)S(1)}, bf16[144,1536]{1,0:T(8,128)(2,1)S(1)}, u32[]{:S(2)}, u32[]{:S(2)}) collective-permute-start(bf16[144,1536]{1,0:T(8,128)(2,1)S(1)} %constant_dynamic-update-slice_fusion.refs_1_), channel_id=1, source_target_pairs={{0,6},{2,0},{4,2},{6,4},{1,7},{3,1},{5,3},{7,5},{8,14},{10,8},{12,... | collective-permute-start | bytes 1327112 | tf_op jit(solution)/shard_map/ppermute | solution.py:27
  41.1 19.3 %collective-permute-start.5 = (bf16[144,1536]{1,0:T(8,128)(2,1)S(1)}, bf16[144,1536]{1,0:T(8,128)(2,1)S(1)}, u32[]{:S(2)}, u32[]{:S(2)}) collective-permute-start(bf16[144,1536]{1,0:T(8,128)(2,1)S(1)} %constant_dynamic-update-slice_fusion.refs_1_), channel_id=1, source_target_pairs={{0,4},{2,6},{4,0},{6,2},{1,5},{3,7},{5,1},{7,3},{8,12},{10,14},{12... | collective-permute-start | bytes 1327112 | tf_op jit(solution)/shard_map/ppermute | solution.py:27
  49.8 27.0 %collective-permute-start.20 = (bf16[384,1536]{1,0:T(8,128)(2,1)S(1)}, bf16[384,1536]{1,0:T(8,128)(2,1)S(1)}, u32[]{:S(2)}, u32[]{:S(2)}) collective-permute-start(bf16[384,1536]{1,0:T(8,128)(2,1)S(1)} %multiply_convert_fusion.refs_5_.refs_6_), channel_id=1, source_target_pairs={{0,32},{32,64},{64,96},{96,0},{1,33},{33,65},{65,97},{97,1},{2,34}... | collective-permute-start | bytes 3538952 | tf_op jit(solution)/shard_map/ppermute | solution.py:27
  51.5 25.5 %collective-permute-start.22 = (bf16[384,1536]{1,0:T(8,128)(2,1)S(1)}, bf16[384,1536]{1,0:T(8,128)(2,1)S(1)}, u32[]{:S(2)}, u32[]{:S(2)}) collective-permute-start(bf16[384,1536]{1,0:T(8,128)(2,1)S(1)} %multiply_convert_fusion.refs_5_.refs_6_), channel_id=1, source_target_pairs={{0,96},{32,0},{64,32},{96,64},{1,97},{33,1},{65,33},{97,65},{2,98}... | collective-permute-start | bytes 3538952 | tf_op jit(solution)/shard_map/ppermute | solution.py:27
  60.4 6.0 %collective-permute-start.6 = (bf16[144,1536]{1,0:T(8,128)(2,1)S(1)}, bf16[144,1536]{1,0:T(8,128)(2,1)S(1)}, u32[]{:S(2)}, u32[]{:S(2)}) collective-permute-start(bf16[144,1536]{1,0:T(8,128)(2,1)S(1)} %constant_dynamic-update-slice_fusion.refs_1_), channel_id=1, source_target_pairs={{0,1},{1,0},{2,3},{3,2},{4,5},{5,4},{6,7},{7,6},{8,9},{9,8},{10,11... | collective-permute-start | bytes 1327112 | tf_op jit(solution)/shard_map/ppermute | solution.py:27
  65.0 2.0 %collective-permute-start.7 = (bf16[144,1536]{1,0:T(8,128)(2,1)S(1)}, bf16[144,1536]{1,0:T(8,128)(2,1)S(1)}, u32[]{:S(2)}, u32[]{:S(2)}) collective-permute-start(bf16[144,1536]{1,0:T(8,128)(2,1)S(1)} %collective-permute-done.3.refs_2_), channel_id=1, source_target_pairs={{0,1},{1,0},{2,3},{3,2},{4,5},{5,4},{6,7},{7,6},{8,9},{9,8},{10,11... | collective-permute-start | bytes 1327112 | tf_op jit(solution)/shard_map/ppermute | solution.py:27
  65.1 4.0 %collective-permute-start.8 = (bf16[144,1536]{1,0:T(8,128)(2,1)S(1)}, bf16[144,1536]{1,0:T(8,128)(2,1)S(1)}, u32[]{:S(2)}, u32[]{:S(2)}) collective-permute-start(bf16[144,1536]{1,0:T(8,128)(2,1)S(1)} %collective-permute-done.4.refs_3_), channel_id=1, source_target_pairs={{0,1},{1,0},{2,3},{3,2},{4,5},{5,4},{6,7},{7,6},{8,9},{9,8},{10,11... | collective-permute-start | bytes 1327112 | tf_op jit(solution)/shard_map/ppermute | solution.py:27
  66.5 16.1 %collective-permute-start.12 = (bf16[192,1536]{1,0:T(8,128)(2,1)S(1)}, bf16[192,1536]{1,0:T(8,128)(2,1)S(1)}, u32[]{:S(2)}, u32[]{:S(2)}) collective-permute-start(bf16[192,1536]{1,0:T(8,128)(2,1)S(1)} %slice.28), channel_id=1, source_target_pairs={{0,8},{8,16},{16,24},{24,0},{1,9},{9,17},{17,25},{25,1},{2,10},{10... | collective-permute-start | bytes 1769480 | tf_op jit(solution)/shard_map/ppermute | solution.py:27
  67.1 15.5 %collective-permute-start.13 = (bf16[192,1536]{1,0:T(8,128)(2,1)S(1)}, bf16[192,1536]{1,0:T(8,128)(2,1)S(1)}, u32[]{:S(2)}, u32[]{:S(2)}) collective-permute-start(bf16[192,1536]{1,0:T(8,128)(2,1)S(1)} %slice.29), channel_id=1, source_target_pairs={{0,24},{8,0},{16,8},{24,16},{1,25},{9,1},{17,9},{25,17},{2,26},{10... | collective-permute-start | bytes 1769480 | tf_op jit(solution)/shard_map/ppermute | solution.py:27
  69.2 2.4 %collective-permute-start.9 = (bf16[144,1536]{1,0:T(8,128)(2,1)S(1)}, bf16[144,1536]{1,0:T(8,128)(2,1)S(1)}, u32[]{:S(2)}, u32[]{:S(2)}) collective-permute-start(bf16[144,1536]{1,0:T(8,128)(2,1)S(1)} %collective-permute-done.5.refs_4_), channel_id=1, source_target_pairs={{0,1},{1,0},{2,3},{3,2},{4,5},{5,4},{6,7},{7,6},{8,9},{9,8},{10,11... | collective-permute-start | bytes 1327112 | tf_op jit(solution)/shard_map/ppermute | solution.py:27
  76.8 18.7 %collective-permute-start.21 = (bf16[192,1536]{1,0:T(8,128)(2,1)S(1)}, bf16[192,1536]{1,0:T(8,128)(2,1)S(1)}, u32[]{:S(2)}, u32[]{:S(2)}) collective-permute-start(bf16[192,1536]{1,0:T(8,128)(2,1)S(1)} %slice.30), channel_id=1, source_target_pairs={{0,32},{32,64},{64,96},{96,0},{1,33},{33,65},{65,97},{97,1},{2,34}... | collective-permute-start | bytes 1769480 | tf_op jit(solution)/shard_map/ppermute | solution.py:27
  77.0 19.9 %collective-permute-start.23 = (bf16[192,1536]{1,0:T(8,128)(2,1)S(1)}, bf16[192,1536]{1,0:T(8,128)(2,1)S(1)}, u32[]{:S(2)}, u32[]{:S(2)}) collective-permute-start(bf16[192,1536]{1,0:T(8,128)(2,1)S(1)} %slice.31), channel_id=1, source_target_pairs={{0,96},{32,0},{64,32},{96,64},{1,97},{33,1},{65,33},{97,65},{2,98}... | collective-permute-start | bytes 1769480 | tf_op jit(solution)/shard_map/ppermute | solution.py:27
  84.2 23.1 %collective-permute-start.14 = (bf16[192,1536]{1,0:T(8,128)(2,1)S(1)}, bf16[192,1536]{1,0:T(8,128)(2,1)S(1)}, u32[]{:S(2)}, u32[]{:S(2)}) collective-permute-start(bf16[192,1536]{1,0:T(8,128)(2,1)S(1)} %get-tuple-element.50), channel_id=1, source_target_pairs={{0,32},{32,64},{64,96},{96,0},{1,33},{33,65},{65,97},{97,1},{2,34}... | collective-permute-start | bytes 1769480 | tf_op jit(solution)/shard_map/ppermute | solution.py:27
  92.7 37.4 %collective-permute-start.16 = (bf16[192,1536]{1,0:T(8,128)(2,1)S(1)}, bf16[192,1536]{1,0:T(8,128)(2,1)S(1)}, u32[]{:S(2)}, u32[]{:S(2)}) collective-permute-start(bf16[192,1536]{1,0:T(8,128)(2,1)S(1)} %get-tuple-element.51), channel_id=1, source_target_pairs={{0,32},{32,64},{64,96},{96,0},{1,33},{33,65},{65,97},{97,1},{2,34}... | collective-permute-start | bytes 1769480 | tf_op jit(solution)/shard_map/ppermute | solution.py:27
  93.4 36.9 %collective-permute-start.17 = (bf16[192,1536]{1,0:T(8,128)(2,1)S(1)}, bf16[192,1536]{1,0:T(8,128)(2,1)S(1)}, u32[]{:S(2)}, u32[]{:S(2)}) collective-permute-start(bf16[192,1536]{1,0:T(8,128)(2,1)S(1)} %get-tuple-element.52), channel_id=1, source_target_pairs={{0,96},{32,0},{64,32},{96,64},{1,97},{33,1},{65,33},{97,65},{2,98}... | collective-permute-start | bytes 1769480 | tf_op jit(solution)/shard_map/ppermute | solution.py:27
  95.5 20.8 %collective-permute-start.18 = (bf16[192,1536]{1,0:T(8,128)(2,1)S(1)}, bf16[192,1536]{1,0:T(8,128)(2,1)S(1)}, u32[]{:S(2)}, u32[]{:S(2)}) collective-permute-start(bf16[192,1536]{1,0:T(8,128)(2,1)S(1)} %get-tuple-element.54), channel_id=1, source_target_pairs={{0,96},{32,0},{64,32},{96,64},{1,97},{33,1},{65,33},{97,65},{2,98}... | collective-permute-start | bytes 1769480 | tf_op jit(solution)/shard_map/ppermute | solution.py:27
  102.3 55.1 %collective-permute-start.26 = (bf16[192,1536]{1,0:T(8,128)(2,1)}, bf16[192,1536]{1,0:T(8,128)(2,1)}, u32[]{:S(2)}, u32[]{:S(2)}) collective-permute-start(bf16[192,1536]{1,0:T(8,128)(2,1)} %get-tuple-element.62), channel_id=1, source_target_pairs={{0,24},{8,0},{16,8},{24,16},{1,25},{9,1},{17,9},{25,17},{2,26},{10... | collective-permute-start | bytes 1769480 | tf_op jit(solution)/shard_map/ppermute | solution.py:27
  107.2 11.1 %collective-permute-start.24 = (bf16[192,1536]{1,0:T(8,128)(2,1)S(1)}, bf16[192,1536]{1,0:T(8,128)(2,1)S(1)}, u32[]{:S(2)}, u32[]{:S(2)}) collective-permute-start(bf16[192,1536]{1,0:T(8,128)(2,1)S(1)} %get-tuple-element.61), channel_id=1, source_target_pairs={{0,8},{8,16},{16,24},{24,0},{1,9},{9,17},{17,25},{25,1},{2,10},{10... | collective-permute-start | bytes 1769480 | tf_op jit(solution)/shard_map/ppermute | solution.py:27
  116.3 9.4 %collective-permute-start.28 = (bf16[192,1536]{1,0:T(8,128)(2,1)S(1)}, bf16[192,1536]{1,0:T(8,128)(2,1)S(1)}, u32[]{:S(2)}, u32[]{:S(2)}) collective-permute-start(bf16[192,1536]{1,0:T(8,128)(2,1)S(1)} %get-tuple-element.65), channel_id=1, source_target_pairs={{0,24},{8,0},{16,8},{24,16},{1,25},{9,1},{17,9},{25,17},{2,26},{10... | collective-permute-start | bytes 1769480 | tf_op jit(solution)/shard_map/ppermute | solution.py:27
  118.3 13.4 %collective-permute-start.15 = (bf16[192,1536]{1,0:T(8,128)(2,1)S(1)}, bf16[192,1536]{1,0:T(8,128)(2,1)S(1)}, u32[]{:S(2)}, u32[]{:S(2)}) collective-permute-start(bf16[192,1536]{1,0:T(8,128)(2,1)S(1)} %add_convert_fusion.3), channel_id=1, source_target_pairs={{0,32},{32,64},{64,96},{96,0},{1,33},{33,65},{65,97},{97,1},{2,34}... | collective-permute-start | bytes 1769480 | tf_op jit(solution)/shard_map/ppermute | solution.py:27
  125.7 10.3 %collective-permute-start.19 = (bf16[192,1536]{1,0:T(8,128)(2,1)S(1)}, bf16[192,1536]{1,0:T(8,128)(2,1)S(1)}, u32[]{:S(2)}, u32[]{:S(2)}) collective-permute-start(bf16[192,1536]{1,0:T(8,128)(2,1)S(1)} %add_convert_fusion.2), channel_id=1, source_target_pairs={{0,96},{32,0},{64,32},{96,64},{1,97},{33,1},{65,33},{97,65},{2,98}... | collective-permute-start | bytes 1769480 | tf_op jit(solution)/shard_map/ppermute | solution.py:27
  130.1 27.3 %collective-permute-start.27 = (bf16[192,1536]{1,0:T(8,128)(2,1)S(1)}, bf16[192,1536]{1,0:T(8,128)(2,1)}, u32[]{:S(2)}, u32[]{:S(2)}) collective-permute-start(bf16[192,1536]{1,0:T(8,128)(2,1)S(1)} %get-tuple-element.63), channel_id=1, source_target_pairs={{0,8},{8,16},{16,24},{24,0},{1,9},{9,17},{17,25},{25,1},{2,10},{10... | collective-permute-start | bytes 1769480 | tf_op jit(solution)/shard_map/ppermute | solution.py:27
  130.3 27.1 %collective-permute-start.25 = (bf16[192,1536]{1,0:T(8,128)(2,1)}, bf16[192,1536]{1,0:T(8,128)(2,1)}, u32[]{:S(2)}, u32[]{:S(2)}) collective-permute-start(bf16[192,1536]{1,0:T(8,128)(2,1)} %add_convert_fusion.1), channel_id=1, source_target_pairs={{0,8},{8,16},{16,24},{24,0},{1,9},{9,17},{17,25},{25,1},{2,10},{10... | collective-permute-start | bytes 1769480 | tf_op jit(solution)/shard_map/ppermute | solution.py:27
  131.7 25.7 %collective-permute-start.29 = (bf16[192,1536]{1,0:T(8,128)(2,1)}, bf16[192,1536]{1,0:T(8,128)(2,1)}, u32[]{:S(2)}, u32[]{:S(2)}) collective-permute-start(bf16[192,1536]{1,0:T(8,128)(2,1)} %add_convert_fusion), channel_id=1, source_target_pairs={{0,24},{8,0},{16,8},{24,16},{1,25},{9,1},{17,9},{25,17},{2,26},{10... | collective-permute-start | bytes 1769480 | tf_op jit(solution)/shard_map/ppermute | solution.py:27
  138.0 28.9 %all-to-all-start = ((f32[128,1,128]{2,1,0:T(1,128)}), f32[128,1,128]{2,1,0:T(1,128)S(1)}, u32[]{:S(2)}, u32[]{:S(2)}) async-start(f32[128,1,128]{2,1,0:T(1,128)} %bitcast.1), calls=%async_computation | async-start | bytes 131072 | tf_op jit(solution)/shard_map/all_to_all | solution.py:451
  175.3 8.7 %all-to-all-start.1 = ((f32[8,1,384]{2,1,0:T(1,128)}), f32[8,1,384]{2,1,0:T(1,128)S(1)}, u32[]{:S(2)}, u32[]{:S(2)}) async-start(f32[8,1,384]{2,1,0:T(1,128)} %get-tuple-element.72), calls=%async_computation.1 | async-start | bytes 24576 | tf_op jit(solution)/shard_map/all_to_all | solution.py:460
  (4 other events, 82.2 us)
where the time goes:
time: 186 us
  waiting for transfers between devices  74.1 us (40%)
  starting transfers between devices  65.3 us (35%)
  Pallas kernels  38.5 us (21%)
  other arithmetic  6.16 us (3%)
    ppermute x30, waiting for transfers between devices, shift(): return lax.ppermute(v, axis, [(i, (i + by) % n) for i in range(n)])  63.6 us
    ppermute x30, starting transfers between devices, shift(): return lax.ppermute(v, axis, [(i, (i + by) % n) for i in range(n)])  42 us
    all_to_all x1, starting transfers between devices, step(): pairs = lax.all_to_all(pair, ALL, 0, 0, tiled=True)  19.4 us
    pallas_call x3, Pallas kernels, input_grad(): pl.pallas_call(functools.partial(input_grad_kernel, len(blocks), own), gr...  11.2 us
    pallas_call x1, Pallas kernels, weight_grad(): pl.pallas_call(functools.partial(weight_grad_kernel, blocks, width), grid...  8.42 us
    pallas_call x1, Pallas kernels, adam(): pl.pallas_call(adam_kernel, grid=(S // ROWS,), in_specs=[pl.BlockSpec((12...  8.35 us
    all_to_all x1, waiting for transfers between devices, step(): pairs = lax.all_to_all(pair, ALL, 0, 0, tiled=True)  6.37 us
    all_to_all x1, waiting for transfers between devices, step(): highs = lax.all_to_all(high, TENSOR, 0, 0, tiled=True)  4.07 us
  transfers between devices with their start and end apart: 32, of which 12 were waited for; matrix products, arithmetic and copies ran while one was open for 3% of the time, Pallas kernels for 15%

commit v1 on v0

--- a/solution.py
+++ b/solution.py
@@ -273,7 +273,7 @@
             pl.BlockSpec((S, C), lambda i: (0, 0)),
             pl.BlockSpec((128, 128), lambda i: (0, 0)),
         ],
-        out_shape=[pltpu.HBM((S, C), F32), jax.ShapeDtypeStruct((128, 128), F32)],
+        out_shape=[pltpu.HBM((S, C), F32), pltpu.HBM((128, 128), F32)],
         compiler_params=params(24),
         name="fold_grad",
     )(*args)
@@ -349,7 +349,7 @@
 
 def input_grad(rows, blocks, weights, own):
     half = jax.ShapeDtypeStruct((HALF, C), BF)
-    outs = [jax.ShapeDtypeStruct((S, C), F32)] if own else [half] * (2 * len(blocks))
+    outs = [pltpu.HBM((S, C), F32)] if own else [half] * (2 * len(blocks))
 
     def piece(k):
         return pl.BlockSpec((1, S, C), lambda i: (k, 0, 0))
@@ -446,18 +446,17 @@
     top = i_own[:HALF] + left_a.astype(F32) + right_a.astype(F32)
     bottom = i_own[HALF:] + left_b.astype(F32) + right_b.astype(F32)
     grad_input = jnp.concatenate([top, bottom], axis=0).astype(BF)
-
     gradient, pair = fold_grad(parts, CHUNKS, peaks)
     pairs = lax.all_to_all(pair, ALL, 0, 0, tiled=True)
     gradient, moment, second, master = (
         pltpu.with_memory_space_constraint(v, pltpu.HBM)
         for v in (gradient, moment, second, master)
     )
-    pairs, grad_input = lax.optimization_barrier((pairs, grad_input))
     new_moment, new_second, new_master, high, peak, again = adam(
         pairs, gradient, moment, second, master
     )
     highs = lax.all_to_all(high, TENSOR, 0, 0, tiled=True)
+    highs, grad_input = lax.optimization_barrier((highs, grad_input))
     new_codes, row_peak = codes(highs, pltpu.with_memory_space_constraint(again, pltpu.VMEM))
     new_scales = row_peak[0].astype(BF)
     return (grad_input, new_master, new_moment, new_second, new_codes, new_scales, peak[0, 64])

time: 186 us -> 189 us (1.016)
  starting transfers between devices: 65.3 us -> 62.8 us
  other arithmetic: 6.16 us -> 8.39 us
  waiting for transfers between devices: 74.1 us -> 76.3 us
    all_to_all x1, starting transfers between devices: 19.4 us -> 13.7 us  [step(): pairs = lax.all_to_all(pair, ALL, 0, 0, tiled=True)]
    ppermute x30, waiting for transfers between devices: 63.6 us -> 68.7 us  [shift(): return lax.ppermute(v, axis, [(i, (i + by) % n) for i in range(n)])]
    ppermute x30, starting transfers between devices: 42 us -> 45.1 us  [shift(): return lax.ppermute(v, axis, [(i, (i + by) % n) for i in range(n)])]
    all_to_all x1, waiting for transfers between devices: 4.07 us -> 1.92 us  [step(): highs = lax.all_to_all(high, TENSOR, 0, 0, tiled=True)]
  transfers between devices with their start and end apart: 32 -> 32, of which waited for: 12 -> 11; matrix products, arithmetic and copies ran while one was open for 3% -> 5% of each run, Pallas kernels for 15% -> 15%
where the time goes in v1:
time: 189 us
  waiting for transfers between devices  76.3 us (40%)
  starting transfers between devices  62.8 us (33%)
  Pallas kernels  39.2 us (21%)
  other arithmetic  8.39 us (4%)
    ppermute x30, waiting for transfers between devices, shift(): return lax.ppermute(v, axis, [(i, (i + by) % n) for i in range(n)])  68.7 us
    ppermute x30, starting transfers between devices, shift(): return lax.ppermute(v, axis, [(i, (i + by) % n) for i in range(n)])  45.1 us
    all_to_all x1, starting transfers between devices, step(): pairs = lax.all_to_all(pair, ALL, 0, 0, tiled=True)  13.7 us
    pallas_call x3, Pallas kernels, input_grad(): pl.pallas_call(functools.partial(input_grad_kernel, len(blocks), own), gr...  11.8 us
    pallas_call x1, Pallas kernels, weight_grad(): pl.pallas_call(functools.partial(weight_grad_kernel, blocks, width), grid...  8.42 us
    pallas_call x1, Pallas kernels, adam(): pl.pallas_call(adam_kernel, grid=(S // ROWS,), in_specs=[pl.BlockSpec((12...  8.35 us
    all_to_all x1, waiting for transfers between devices, step(): pairs = lax.all_to_all(pair, ALL, 0, 0, tiled=True)  5.63 us
    all_to_all x1, starting transfers between devices, step(): highs = lax.all_to_all(high, TENSOR, 0, 0, tiled=True)  4 us
  transfers between devices with their start and end apart: 32, of which 11 were waited for; matrix products, arithmetic and copies ran while one was open for 5% of the time, Pallas kernels for 15%

profile of v1, /device:TPU:1, one launch (start us, length us, event | category | flops | bytes accessed | tf_op | source)
XLA Modules:
  0.0 189.1 jit_solution(11704430134095686863)
XLA Ops:
  2.0 2.1 %collective-permute-start = (bf16[48,1536]{1,0:T(8,128)(2,1)S(1)}, bf16[48,1536]{1,0:T(8,128)(2,1)S(1)}, u32[]{:S(2)}, u32[]{:S(2)}) collective-permute-start(bf16[48,1536]{1,0:T(8,128)(2,1)S(1)} %get-tuple-element.42), channel_id=1, source_target_pairs={{0,8},{8,16},{16,24},{24,0},{1,9},{9,17},{17,25},{25,1},{2,10},{10... | collective-permute-start | bytes 442376 | tf_op jit(solution)/shard_map/ppermute | solution.py:27
  5.5 2.6 %collective-permute-start.1 = (bf16[48,1536]{1,0:T(8,128)(2,1)S(1)}, bf16[48,1536]{1,0:T(8,128)(2,1)S(1)}, u32[]{:S(2)}, u32[]{:S(2)}) collective-permute-start(bf16[48,1536]{1,0:T(8,128)(2,1)S(1)} %get-tuple-element.43), channel_id=1, source_target_pairs={{0,24},{8,0},{16,8},{24,16},{1,25},{9,1},{17,9},{25,17},{2,26},{10... | collective-permute-start | bytes 442376 | tf_op jit(solution)/shard_map/ppermute | solution.py:27
  8.6 25.2 %collective-permute-done.1 = bf16[48,1536]{1,0:T(8,128)(2,1)S(1)} collective-permute-done((bf16[48,1536]{1,0:T(8,128)(2,1)S(1)}, bf16[48,1536]{1,0:T(8,128)(2,1)S(1)}, u32[]{:S(2)}, u32[]{:S(2)}) %collective-permute-start.1) | collective-permute-done | bytes 147488 | tf_op jit(solution)/shard_map/ppermute | solution.py:27
  33.8 4.4 %collective-permute-done.2 = bf16[48,1536]{1,0:T(8,128)(2,1)S(1)} collective-permute-done((bf16[48,1536]{1,0:T(8,128)(2,1)S(1)}, bf16[48,1536]{1,0:T(8,128)(2,1)S(1)}, u32[]{:S(2)}, u32[]{:S(2)}) %collective-permute-start.2) | collective-permute-done | bytes 147488 | tf_op jit(solution)/shard_map/ppermute | solution.py:27
  39.8 2.9 %collective-permute-start.5 = (bf16[144,1536]{1,0:T(8,128)(2,1)S(1)}, bf16[144,1536]{1,0:T(8,128)(2,1)S(1)}, u32[]{:S(2)}, u32[]{:S(2)}) collective-permute-start(bf16[144,1536]{1,0:T(8,128)(2,1)S(1)} %constant_dynamic-update-slice_fusion.refs_1_), channel_id=1, source_target_pairs={{0,4},{2,6},{4,0},{6,2},{1,5},{3,7},{5,1},{7,3},{8,12},{10,14},{12... | collective-permute-start | bytes 1327112 | tf_op jit(solution)/shard_map/ppermute | solution.py:27
  43.8 3.8 %collective-permute-start.22 = (bf16[384,1536]{1,0:T(8,128)(2,1)S(1)}, bf16[384,1536]{1,0:T(8,128)(2,1)S(1)}, u32[]{:S(2)}, u32[]{:S(2)}) collective-permute-start(bf16[384,1536]{1,0:T(8,128)(2,1)S(1)} %multiply_convert_fusion.refs_5_.refs_6_), channel_id=1, source_target_pairs={{0,96},{32,0},{64,32},{96,64},{1,97},{33,1},{65,33},{97,65},{2,98}... | collective-permute-start | bytes 3538952 | tf_op jit(solution)/shard_map/ppermute | solution.py:27
  47.6 5.3 %collective-permute-done.5.refs_4_ = bf16[144,1536]{1,0:T(8,128)(2,1)S(1)} collective-permute-done((bf16[144,1536]{1,0:T(8,128)(2,1)S(1)}, bf16[144,1536]{1,0:T(8,128)(2,1)S(1)}, u32[]{:S(2)}, u32[]{:S(2)}) %collective-permute-start.5) | collective-permute-done | bytes 442400 | tf_op jit(solution)/shard_map/ppermute | solution.py:27
  54.6 8.2 %collective-permute-done.4.refs_3_ = bf16[144,1536]{1,0:T(8,128)(2,1)S(1)} collective-permute-done((bf16[144,1536]{1,0:T(8,128)(2,1)S(1)}, bf16[144,1536]{1,0:T(8,128)(2,1)S(1)}, u32[]{:S(2)}, u32[]{:S(2)}) %collective-permute-start.4) | collective-permute-done | bytes 442400 | tf_op jit(solution)/shard_map/ppermute | solution.py:27
  65.2 10.0 %collective-permute-done.3.refs_2_ = bf16[144,1536]{1,0:T(8,128)(2,1)S(1)} collective-permute-done((bf16[144,1536]{1,0:T(8,128)(2,1)S(1)}, bf16[144,1536]{1,0:T(8,128)(2,1)S(1)}, u32[]{:S(2)}, u32[]{:S(2)}) %collective-permute-start.3) | collective-permute-done | bytes 442400 | tf_op jit(solution)/shard_map/ppermute | solution.py:27
  76.9 2.0 %collective-permute-start.7 = (bf16[144,1536]{1,0:T(8,128)(2,1)S(1)}, bf16[144,1536]{1,0:T(8,128)(2,1)S(1)}, u32[]{:S(2)}, u32[]{:S(2)}) collective-permute-start(bf16[144,1536]{1,0:T(8,128)(2,1)S(1)} %collective-permute-done.3.refs_2_), channel_id=1, source_target_pairs={{0,1},{1,0},{2,3},{3,2},{4,5},{5,4},{6,7},{7,6},{8,9},{9,8},{10,11... | collective-permute-start | bytes 1327112 | tf_op jit(solution)/shard_map/ppermute | solution.py:27
  82.0 3.8 %collective-permute-start.23 = (bf16[192,1536]{1,0:T(8,128)(2,1)S(1)}, bf16[192,1536]{1,0:T(8,128)(2,1)S(1)}, u32[]{:S(2)}, u32[]{:S(2)}) collective-permute-start(bf16[192,1536]{1,0:T(8,128)(2,1)S(1)} %slice.31), channel_id=1, source_target_pairs={{0,96},{32,0},{64,32},{96,64},{1,97},{33,1},{65,33},{97,65},{2,98}... | collective-permute-start | bytes 1769480 | tf_op jit(solution)/shard_map/ppermute | solution.py:27
  85.9 2.8 %far_start.1 = (f32[384,1536]{1,0:T(8,128)S(1)}, f32[8,256]{1,0:T(8,128)S(1)}) custom-call(bf16[4,384,1536]{2,1,0:T(8,128)(2,1)S(1)} %get-tuple-element.45.refs_0_.refs_1_.refs_2_.cols_ref, bf16[384,1536]{1,0:T(8,128)(2,1)S(1)} %copy-done.1, bf16[384,1536]{1,0:T(8,128)(2,1)S(1)} %collective-permute-done.10.refs_4_.left_ref, ...), custom_call_target="tpu_custom_call" | custom-call | flops 1358954496 | bytes 6291456 | tf_op jit(solution)/shard_map/far_start/pallas_call | solution.py:200
  88.8 2.2 %collective-permute-done.12.refs_6_.top_ref = bf16[192,1536]{1,0:T(8,128)(2,1)S(1)} collective-permute-done((bf16[192,1536]{1,0:T(8,128)(2,1)S(1)}, bf16[192,1536]{1,0:T(8,128)(2,1)S(1)}, u32[]{:S(2)}, u32[]{:S(2)}) %collective-permute-start.12) | collective-permute-done | bytes 589856 | tf_op jit(solution)/shard_map/ppermute | solution.py:27
  94.3 8.4 %weight_grad.1 = (bf16[192,1536]{1,0:T(8,128)(2,1)S(1)}, bf16[192,1536]{1,0:T(8,128)(2,1)S(1)}, bf16[192,1536]{1,0:T(8,128)(2,1)S(1)}, bf16[192,1536]{1,0:T(8,12...) custom-call(bf16[4,384,1536]{2,1,0:T(8,128)(2,1)S(1)} %get-tuple-element.45.refs_0_.refs_1_.refs_2_.cols_ref, ...), custom_call_target="tpu_custom_call" | custom-call | flops 5435817984 | bytes 9437184 | tf_op jit(solution)/shard_map/weight_grad/pallas_call | solution.py:143
  102.8 2.2 %collective-permute-start.18 = (bf16[192,1536]{1,0:T(8,128)(2,1)S(1)}, bf16[192,1536]{1,0:T(8,128)(2,1)S(1)}, u32[]{:S(2)}, u32[]{:S(2)}) collective-permute-start(bf16[192,1536]{1,0:T(8,128)(2,1)S(1)} %get-tuple-element.54), channel_id=1, source_target_pairs={{0,96},{32,0},{64,32},{96,64},{1,97},{33,1},{65,33},{97,65},{2,98}... | collective-permute-start | bytes 1769480 | tf_op jit(solution)/shard_map/ppermute | solution.py:27
  105.0 2.7 %collective-permute-start.17 = (bf16[192,1536]{1,0:T(8,128)(2,1)S(1)}, bf16[192,1536]{1,0:T(8,128)(2,1)S(1)}, u32[]{:S(2)}, u32[]{:S(2)}) collective-permute-start(bf16[192,1536]{1,0:T(8,128)(2,1)S(1)} %get-tuple-element.52), channel_id=1, source_target_pairs={{0,96},{32,0},{64,32},{96,64},{1,97},{33,1},{65,33},{97,65},{2,98}... | collective-permute-start | bytes 1769480 | tf_op jit(solution)/shard_map/ppermute | solution.py:27
  107.6 2.9 %input_grad.5 = (bf16[192,1536]{1,0:T(8,128)(2,1)S(1)}, bf16[192,1536]{1,0:T(8,128)(2,1)S(1)}) custom-call(bf16[4,384,1536]{2,1,0:T(8,128)(2,1)S(1)} %get-tuple-element.61.refs_0_.refs_1_, bf16[192,1536]{1,0:T(8,128)(2,1)S(1)} %collective-permute-done.21.refs_1_.refs_2_, bf16[192,1536]{1,0:T(8,128)(2,1)S(1)} %collective-permute-done.23.refs_2_.refs_3_, ...), custom_call_target="tpu_custom_call" | custom-call | flops 1811939328 | bytes 9437184 | tf_op jit(solution)/shard_map/input_grad/pallas_call | solution.py:360
  110.8 4.7 %input_grad.4 = (bf16[192,1536]{1,0:T(8,128)(2,1)S(1)}, bf16[192,1536]{1,0:T(8,128)(2,1)S(1)}, bf16[192,1536]{1,0:T(8,128)(2,1)S(1)}, bf16[192,1536]{1,0:T(8,128)(2,1)S(1)}) custom-call(bf16[4,384,1536]{2,1,0:T(8,128)(2,1)S(1)} %get-tuple-element.61.refs_0_.refs_1_, bf16[4,384,1536]{2,1,0:T(8,128)(2,1)S(1)} %get-tuple-element.61.refs_0_.refs_1_, ...), custom_call_target="tpu_custom_call" | custom-call | flops 3623878656 | bytes 9437184 | tf_op jit(solution)/shard_map/input_grad/pallas_call | solution.py:360
  115.5 2.7 %collective-permute-start.28 = (bf16[192,1536]{1,0:T(8,128)(2,1)S(1)}, bf16[192,1536]{1,0:T(8,128)(2,1)S(1)}, u32[]{:S(2)}, u32[]{:S(2)}) collective-permute-start(bf16[192,1536]{1,0:T(8,128)(2,1)S(1)} %get-tuple-element.67), channel_id=1, source_target_pairs={{0,24},{8,0},{16,8},{24,16},{1,25},{9,1},{17,9},{25,17},{2,26},{10... | collective-permute-start | bytes 1769480 | tf_op jit(solution)/shard_map/ppermute | solution.py:27
  118.6 8.4 %collective-permute-done.28 = bf16[192,1536]{1,0:T(8,128)(2,1)S(1)} collective-permute-done((bf16[192,1536]{1,0:T(8,128)(2,1)S(1)}, bf16[192,1536]{1,0:T(8,128)(2,1)S(1)}, u32[]{:S(2)}, u32[]{:S(2)}) %collective-permute-start.28) | collective-permute-done | bytes 589856 | tf_op jit(solution)/shard_map/ppermute | solution.py:27
  127.9 2.7 %collective-permute-start.19 = (bf16[192,1536]{1,0:T(8,128)(2,1)S(1)}, bf16[192,1536]{1,0:T(8,128)(2,1)S(1)}, u32[]{:S(2)}, u32[]{:S(2)}) collective-permute-start(bf16[192,1536]{1,0:T(8,128)(2,1)S(1)} %add_convert_fusion.2), channel_id=1, source_target_pairs={{0,96},{32,0},{64,32},{96,64},{1,97},{33,1},{65,33},{97,65},{2,98}... | collective-permute-start | bytes 1769480 | tf_op jit(solution)/shard_map/ppermute | solution.py:27
  133.4 3.5 %collective-permute-done.15.refs_1_ = bf16[192,1536]{1,0:T(8,128)(2,1)S(1)} collective-permute-done((bf16[192,1536]{1,0:T(8,128)(2,1)S(1)}, bf16[192,1536]{1,0:T(8,128)(2,1)S(1)}, u32[]{:S(2)}, u32[]{:S(2)}) %collective-permute-start.15) | collective-permute-done | bytes 589856 | tf_op jit(solution)/shard_map/ppermute | solution.py:27
  136.9 3.7 %collective-permute-start.29 = (bf16[192,1536]{1,0:T(8,128)(2,1)}, bf16[192,1536]{1,0:T(8,128)(2,1)}, u32[]{:S(2)}, u32[]{:S(2)}) collective-permute-start(bf16[192,1536]{1,0:T(8,128)(2,1)} %add_convert_fusion), channel_id=1, source_target_pairs={{0,24},{8,0},{16,8},{24,16},{1,25},{9,1},{17,9},{25,17},{2,26},{10... | collective-permute-start | bytes 1769480 | tf_op jit(solution)/shard_map/ppermute | solution.py:27
  140.6 4.3 %input_grad.3 = f32[384,1536]{1,0:T(8,128)} custom-call(bf16[4,384,1536]{2,1,0:T(8,128)(2,1)S(1)} %get-tuple-element.61.refs_0_.refs_1_, bf16[192,1536]{1,0:T(8,128)(2,1)S(1)} %collective-permute-done.21.refs_1_.refs_2_, bf16[192,1536]{1,0:T(8,128)(2,1)S(1)} %collective-permute-done.23.refs_2_.refs_3_, ...), custom_call_target="tpu_custom_call" | custom-call | flops 1811939328 | bytes 9437184 | tf_op jit(solution)/shard_map/input_grad/pallas_call | solution.py:360
  144.9 2.0 %fold_grad.1 = (f32[384,1536]{1,0:T(8,128)}, f32[128,128]{1,0:T(8,128)}) custom-call(f32[384,1536]{1,0:T(8,128)S(1)} %get-tuple-element.46.refs_0_, bf16[192,1536]{1,0:T(8,128)(2,1)S(1)} %collective-permute-done.15.refs_1_, bf16[192,1536]{1,0:T(8,128)(2,1)S(1)} %collective-permute-done.16.refs_2_, bf16[192,1536]{1,0:T(8,128)(2,1)S(1)} %collective-permute-done.17.refs_3_, ...), custom_call_target="tpu_custom_call" | custom-call | tf_op jit(solution)/shard_map/fold_grad/pallas_call | solution.py:268
  146.9 13.7 %all-to-all-start = ((f32[128,1,128]{2,1,0:T(1,128)}), f32[128,1,128]{2,1,0:T(1,128)S(1)}, u32[]{:S(2)}, u32[]{:S(2)}) async-start(f32[128,1,128]{2,1,0:T(1,128)} %bitcast.6), calls=%async_computation | async-start | bytes 131072 | tf_op jit(solution)/shard_map/all_to_all | solution.py:450
  161.4 3.2 %fusion.3 = (bf16[192,1536]{1,0:T(8,128)(2,1)S(1)}, bf16[192,1536]{1,0:T(8,128)(2,1)}) fusion(f32[384,1536]{1,0:T(8,128)} %input_grad.3, bf16[192,1536]{1,0:T(8,128)(2,1)S(1)} %collective-permute-done.26, bf16[192,1536]{1,0:T(8,128)(2,1)} %copy-done.3, bf16[192,1536]{1,0:T(8,128)(2,1)} %collective-permute-done.29, ...), kind=kLoop, calls=%fused_computation.6 | loop fusion | flops 2949120 | bytes 5898240 | tf_op jit(solution)/shard_map/convert
  164.6 5.6 %all-to-all-done = f32[128,1,128]{2,1,0:T(1,128)S(1)} async-done(((f32[128,1,128]{2,1,0:T(1,128)}), f32[128,1,128]{2,1,0:T(1,128)S(1)}, u32[]{:S(2)}, u32[]{:S(2)}) %all-to-all-start) | async-done | bytes 65568 | tf_op jit(solution)/shard_map/all_to_all | solution.py:450
  170.3 8.3 %adam.1 = (f32[384,1536]{1,0:T(8,128)}, f32[384,1536]{1,0:T(8,128)}, f32[384,1536]{1,0:T(8,128)}, f32[8,1,384]{2,1,0:T(1,128)}, f32[8,128]{1,0:T(8,128)S(1)}, /*index=5*/f32[384,1536]{1,0:T(8,128)S(1)}) custom-call(f32[128,128]{1,0:T(8,128)S(1)} %bitcast.5, f32[384,1536]{1,0:T(8,128)} %get-tuple-element.58.grad_ref, f32[384,1536]{1,0:T(8,128)} %moment_ref.1, ...), custom_call_target="tpu_custom_call" | custom-call | tf_op jit(solution)/shard_map/adam/pallas_call | solution.py:318
  178.6 4.0 %all-to-all-start.1 = ((f32[8,1,384]{2,1,0:T(1,128)}), f32[8,1,384]{2,1,0:T(1,128)S(1)}, u32[]{:S(2)}, u32[]{:S(2)}) async-start(f32[8,1,384]{2,1,0:T(1,128)} %get-tuple-element.59), calls=%async_computation.1 | async-start | bytes 24576 | tf_op jit(solution)/shard_map/all_to_all | solution.py:458
  182.6 2.2 %pad_maximum_fusion = bf16[384,1536]{1,0:T(8,128)(2,1)} fusion(bf16[192,1536]{1,0:T(8,128)(2,1)} %get-tuple-element.78, bf16[192,1536]{1,0:T(8,128)(2,1)S(1)} %get-tuple-element.77), kind=kLoop, calls=%fused_computation.7 | loop fusion | flops 2359296 | bytes 2359296 | tf_op jit(solution)/shard_map/concatenate | solution.py:448
  185.4 1.9 %all-to-all-done.1.highs_ref = f32[8,1,384]{2,1,0:T(1,128)S(1)} async-done(((f32[8,1,384]{2,1,0:T(1,128)}), f32[8,1,384]{2,1,0:T(1,128)S(1)}, u32[]{:S(2)}, u32[]{:S(2)}) %all-to-all-start.1) | async-done | bytes 12320 | tf_op jit(solution)/shard_map/all_to_all | solution.py:458
  (70 shorter events, 25.7 us)
Async XLA Ops:
  2.0 6.6 %collective-permute-start = (bf16[48,1536]{1,0:T(8,128)(2,1)S(1)}, bf16[48,1536]{1,0:T(8,128)(2,1)S(1)}, u32[]{:S(2)}, u32[]{:S(2)}) collective-permute-start(bf16[48,1536]{1,0:T(8,128)(2,1)S(1)} %get-tuple-element.42), channel_id=1, source_target_pairs={{0,8},{8,16},{16,24},{24,0},{1,9},{9,17},{17,25},{25,1},{2,10},{10... | collective-permute-start | bytes 442376 | tf_op jit(solution)/shard_map/ppermute | solution.py:27
  4.1 60.2 %collective-permute-start.11 = (bf16[384,1536]{1,0:T(8,128)(2,1)S(1)}, bf16[384,1536]{1,0:T(8,128)(2,1)S(1)}, u32[]{:S(2)}, u32[]{:S(2)}) collective-permute-start(bf16[384,1536]{1,0:T(8,128)(2,1)S(1)} %copy-done.1), channel_id=1, source_target_pairs={{0,24},{8,0},{16,8},{24,16},{1,25},{9,1},{17,9},{25,17},{2,26},{10... | collective-permute-start | bytes 3538952 | tf_op jit(solution)/shard_map/ppermute | solution.py:27
  5.4 59.6 %collective-permute-start.10 = (bf16[384,1536]{1,0:T(8,128)(2,1)S(1)}, bf16[384,1536]{1,0:T(8,128)(2,1)S(1)}, u32[]{:S(2)}, u32[]{:S(2)}) collective-permute-start(bf16[384,1536]{1,0:T(8,128)(2,1)S(1)} %copy-done.1), channel_id=1, source_target_pairs={{0,8},{8,16},{16,24},{24,0},{1,9},{9,17},{17,25},{25,1},{2,10},{10... | collective-permute-start | bytes 3538952 | tf_op jit(solution)/shard_map/ppermute | solution.py:27
  5.5 28.3 %collective-permute-start.1 = (bf16[48,1536]{1,0:T(8,128)(2,1)S(1)}, bf16[48,1536]{1,0:T(8,128)(2,1)S(1)}, u32[]{:S(2)}, u32[]{:S(2)}) collective-permute-start(bf16[48,1536]{1,0:T(8,128)(2,1)S(1)} %get-tuple-element.43), channel_id=1, source_target_pairs={{0,24},{8,0},{16,8},{24,16},{1,25},{9,1},{17,9},{25,17},{2,26},{10... | collective-permute-start | bytes 442376 | tf_op jit(solution)/shard_map/ppermute | solution.py:27
  8.1 30.1 %collective-permute-start.2 = (bf16[48,1536]{1,0:T(8,128)(2,1)S(1)}, bf16[48,1536]{1,0:T(8,128)(2,1)S(1)}, u32[]{:S(2)}, u32[]{:S(2)}) collective-permute-start(bf16[48,1536]{1,0:T(8,128)(2,1)S(1)} %get-tuple-element.44), channel_id=1, source_target_pairs={{0,16},{8,24},{16,0},{24,8},{1,17},{9,25},{17,1},{25,9},{2,18},{10... | collective-permute-start | bytes 442376 | tf_op jit(solution)/shard_map/ppermute | solution.py:27
  38.2 5.6 %collective-permute-start.6 = (bf16[144,1536]{1,0:T(8,128)(2,1)S(1)}, bf16[144,1536]{1,0:T(8,128)(2,1)S(1)}, u32[]{:S(2)}, u32[]{:S(2)}) collective-permute-start(bf16[144,1536]{1,0:T(8,128)(2,1)S(1)} %constant_dynamic-update-slice_fusion.refs_1_), channel_id=1, source_target_pairs={{0,1},{1,0},{2,3},{3,2},{4,5},{5,4},{6,7},{7,6},{8,9},{9,8},{10,11... | collective-permute-start | bytes 1327112 | tf_op jit(solution)/shard_map/ppermute | solution.py:27
  39.8 13.1 %collective-permute-start.5 = (bf16[144,1536]{1,0:T(8,128)(2,1)S(1)}, bf16[144,1536]{1,0:T(8,128)(2,1)S(1)}, u32[]{:S(2)}, u32[]{:S(2)}) collective-permute-start(bf16[144,1536]{1,0:T(8,128)(2,1)S(1)} %constant_dynamic-update-slice_fusion.refs_1_), channel_id=1, source_target_pairs={{0,4},{2,6},{4,0},{6,2},{1,5},{3,7},{5,1},{7,3},{8,12},{10,14},{12... | collective-permute-start | bytes 1327112 | tf_op jit(solution)/shard_map/ppermute | solution.py:27
  42.8 20.1 %collective-permute-start.4 = (bf16[144,1536]{1,0:T(8,128)(2,1)S(1)}, bf16[144,1536]{1,0:T(8,128)(2,1)S(1)}, u32[]{:S(2)}, u32[]{:S(2)}) collective-permute-start(bf16[144,1536]{1,0:T(8,128)(2,1)S(1)} %constant_dynamic-update-slice_fusion.refs_1_), channel_id=1, source_target_pairs={{0,6},{2,0},{4,2},{6,4},{1,7},{3,1},{5,3},{7,5},{8,14},{10,8},{12,... | collective-permute-start | bytes 1327112 | tf_op jit(solution)/shard_map/ppermute | solution.py:27
  43.8 38.1 %collective-permute-start.22 = (bf16[384,1536]{1,0:T(8,128)(2,1)S(1)}, bf16[384,1536]{1,0:T(8,128)(2,1)S(1)}, u32[]{:S(2)}, u32[]{:S(2)}) collective-permute-start(bf16[384,1536]{1,0:T(8,128)(2,1)S(1)} %multiply_convert_fusion.refs_5_.refs_6_), channel_id=1, source_target_pairs={{0,96},{32,0},{64,32},{96,64},{1,97},{33,1},{65,33},{97,65},{2,98}... | collective-permute-start | bytes 3538952 | tf_op jit(solution)/shard_map/ppermute | solution.py:27
  53.0 32.8 %collective-permute-start.20 = (bf16[384,1536]{1,0:T(8,128)(2,1)S(1)}, bf16[384,1536]{1,0:T(8,128)(2,1)S(1)}, u32[]{:S(2)}, u32[]{:S(2)}) collective-permute-start(bf16[384,1536]{1,0:T(8,128)(2,1)S(1)} %multiply_convert_fusion.refs_5_.refs_6_), channel_id=1, source_target_pairs={{0,32},{32,64},{64,96},{96,0},{1,33},{33,65},{65,97},{97,1},{2,34}... | collective-permute-start | bytes 3538952 | tf_op jit(solution)/shard_map/ppermute | solution.py:27
  62.8 12.3 %collective-permute-start.3 = (bf16[144,1536]{1,0:T(8,128)(2,1)S(1)}, bf16[144,1536]{1,0:T(8,128)(2,1)S(1)}, u32[]{:S(2)}, u32[]{:S(2)}) collective-permute-start(bf16[144,1536]{1,0:T(8,128)(2,1)S(1)} %constant_dynamic-update-slice_fusion.refs_1_), channel_id=1, source_target_pairs={{0,2},{2,4},{4,6},{6,0},{1,3},{3,5},{5,7},{7,1},{8,10},{10,12},{12... | collective-permute-start | bytes 1327112 | tf_op jit(solution)/shard_map/ppermute | solution.py:27
  64.2 12.6 %collective-permute-start.9 = (bf16[144,1536]{1,0:T(8,128)(2,1)S(1)}, bf16[144,1536]{1,0:T(8,128)(2,1)S(1)}, u32[]{:S(2)}, u32[]{:S(2)}) collective-permute-start(bf16[144,1536]{1,0:T(8,128)(2,1)S(1)} %collective-permute-done.5.refs_4_), channel_id=1, source_target_pairs={{0,1},{1,0},{2,3},{3,2},{4,5},{5,4},{6,7},{7,6},{8,9},{9,8},{10,11... | collective-permute-start | bytes 1327112 | tf_op jit(solution)/shard_map/ppermute | solution.py:27
  65.0 11.9 %collective-permute-start.8 = (bf16[144,1536]{1,0:T(8,128)(2,1)S(1)}, bf16[144,1536]{1,0:T(8,128)(2,1)S(1)}, u32[]{:S(2)}, u32[]{:S(2)}) collective-permute-start(bf16[144,1536]{1,0:T(8,128)(2,1)S(1)} %collective-permute-done.4.refs_3_), channel_id=1, source_target_pairs={{0,1},{1,0},{2,3},{3,2},{4,5},{5,4},{6,7},{7,6},{8,9},{9,8},{10,11... | collective-permute-start | bytes 1327112 | tf_op jit(solution)/shard_map/ppermute | solution.py:27
  75.1 13.7 %collective-permute-start.13 = (bf16[192,1536]{1,0:T(8,128)(2,1)S(1)}, bf16[192,1536]{1,0:T(8,128)(2,1)S(1)}, u32[]{:S(2)}, u32[]{:S(2)}) collective-permute-start(bf16[192,1536]{1,0:T(8,128)(2,1)S(1)} %slice.29), channel_id=1, source_target_pairs={{0,24},{8,0},{16,8},{24,16},{1,25},{9,1},{17,9},{25,17},{2,26},{10... | collective-permute-start | bytes 1769480 | tf_op jit(solution)/shard_map/ppermute | solution.py:27
  76.9 14.2 %collective-permute-start.12 = (bf16[192,1536]{1,0:T(8,128)(2,1)S(1)}, bf16[192,1536]{1,0:T(8,128)(2,1)S(1)}, u32[]{:S(2)}, u32[]{:S(2)}) collective-permute-start(bf16[192,1536]{1,0:T(8,128)(2,1)S(1)} %slice.28), channel_id=1, source_target_pairs={{0,8},{8,16},{16,24},{24,0},{1,9},{9,17},{17,25},{25,1},{2,10},{10... | collective-permute-start | bytes 1769480 | tf_op jit(solution)/shard_map/ppermute | solution.py:27
  76.9 3.4 %collective-permute-start.7 = (bf16[144,1536]{1,0:T(8,128)(2,1)S(1)}, bf16[144,1536]{1,0:T(8,128)(2,1)S(1)}, u32[]{:S(2)}, u32[]{:S(2)}) collective-permute-start(bf16[144,1536]{1,0:T(8,128)(2,1)S(1)} %collective-permute-done.3.refs_2_), channel_id=1, source_target_pairs={{0,1},{1,0},{2,3},{3,2},{4,5},{5,4},{6,7},{7,6},{8,9},{9,8},{10,11... | collective-permute-start | bytes 1327112 | tf_op jit(solution)/shard_map/ppermute | solution.py:27
  82.0 23.0 %collective-permute-start.23 = (bf16[192,1536]{1,0:T(8,128)(2,1)S(1)}, bf16[192,1536]{1,0:T(8,128)(2,1)S(1)}, u32[]{:S(2)}, u32[]{:S(2)}) collective-permute-start(bf16[192,1536]{1,0:T(8,128)(2,1)S(1)} %slice.31), channel_id=1, source_target_pairs={{0,96},{32,0},{64,32},{96,64},{1,97},{33,1},{65,33},{97,65},{2,98}... | collective-permute-start | bytes 1769480 | tf_op jit(solution)/shard_map/ppermute | solution.py:27
  85.8 21.8 %collective-permute-start.21 = (bf16[192,1536]{1,0:T(8,128)(2,1)S(1)}, bf16[192,1536]{1,0:T(8,128)(2,1)S(1)}, u32[]{:S(2)}, u32[]{:S(2)}) collective-permute-start(bf16[192,1536]{1,0:T(8,128)(2,1)S(1)} %slice.30), channel_id=1, source_target_pairs={{0,32},{32,64},{64,96},{96,0},{1,33},{33,65},{65,97},{97,1},{2,34}... | collective-permute-start | bytes 1769480 | tf_op jit(solution)/shard_map/ppermute | solution.py:27
  92.6 22.8 %collective-permute-start.14 = (bf16[192,1536]{1,0:T(8,128)(2,1)S(1)}, bf16[192,1536]{1,0:T(8,128)(2,1)S(1)}, u32[]{:S(2)}, u32[]{:S(2)}) collective-permute-start(bf16[192,1536]{1,0:T(8,128)(2,1)S(1)} %get-tuple-element.50), channel_id=1, source_target_pairs={{0,32},{32,64},{64,96},{96,0},{1,33},{33,65},{65,97},{97,1},{2,34}... | collective-permute-start | bytes 1769480 | tf_op jit(solution)/shard_map/ppermute | solution.py:27
  102.8 15.6 %collective-permute-start.18 = (bf16[192,1536]{1,0:T(8,128)(2,1)S(1)}, bf16[192,1536]{1,0:T(8,128)(2,1)S(1)}, u32[]{:S(2)}, u32[]{:S(2)}) collective-permute-start(bf16[192,1536]{1,0:T(8,128)(2,1)S(1)} %get-tuple-element.54), channel_id=1, source_target_pairs={{0,96},{32,0},{64,32},{96,64},{1,97},{33,1},{65,33},{97,65},{2,98}... | collective-permute-start | bytes 1769480 | tf_op jit(solution)/shard_map/ppermute | solution.py:27
  105.0 26.6 %collective-permute-start.16 = (bf16[192,1536]{1,0:T(8,128)(2,1)S(1)}, bf16[192,1536]{1,0:T(8,128)(2,1)S(1)}, u32[]{:S(2)}, u32[]{:S(2)}) collective-permute-start(bf16[192,1536]{1,0:T(8,128)(2,1)S(1)} %get-tuple-element.51), channel_id=1, source_target_pairs={{0,32},{32,64},{64,96},{96,0},{1,33},{33,65},{65,97},{97,1},{2,34}... | collective-permute-start | bytes 1769480 | tf_op jit(solution)/shard_map/ppermute | solution.py:27
  105.0 26.6 %collective-permute-start.17 = (bf16[192,1536]{1,0:T(8,128)(2,1)S(1)}, bf16[192,1536]{1,0:T(8,128)(2,1)S(1)}, u32[]{:S(2)}, u32[]{:S(2)}) collective-permute-start(bf16[192,1536]{1,0:T(8,128)(2,1)S(1)} %get-tuple-element.52), channel_id=1, source_target_pairs={{0,96},{32,0},{64,32},{96,64},{1,97},{33,1},{65,33},{97,65},{2,98}... | collective-permute-start | bytes 1769480 | tf_op jit(solution)/shard_map/ppermute | solution.py:27
  110.5 17.4 %collective-permute-start.24 = (bf16[192,1536]{1,0:T(8,128)(2,1)S(1)}, bf16[192,1536]{1,0:T(8,128)(2,1)S(1)}, u32[]{:S(2)}, u32[]{:S(2)}) collective-permute-start(bf16[192,1536]{1,0:T(8,128)(2,1)S(1)} %get-tuple-element.63), channel_id=1, source_target_pairs={{0,8},{8,16},{16,24},{24,0},{1,9},{9,17},{17,25},{25,1},{2,10},{10... | collective-permute-start | bytes 1769480 | tf_op jit(solution)/shard_map/ppermute | solution.py:27
  115.5 11.5 %collective-permute-start.28 = (bf16[192,1536]{1,0:T(8,128)(2,1)S(1)}, bf16[192,1536]{1,0:T(8,128)(2,1)S(1)}, u32[]{:S(2)}, u32[]{:S(2)}) collective-permute-start(bf16[192,1536]{1,0:T(8,128)(2,1)S(1)} %get-tuple-element.67), channel_id=1, source_target_pairs={{0,24},{8,0},{16,8},{24,16},{1,25},{9,1},{17,9},{25,17},{2,26},{10... | collective-permute-start | bytes 1769480 | tf_op jit(solution)/shard_map/ppermute | solution.py:27
  118.3 42.2 %collective-permute-start.26 = (bf16[192,1536]{1,0:T(8,128)(2,1)S(1)}, bf16[192,1536]{1,0:T(8,128)(2,1)S(1)}, u32[]{:S(2)}, u32[]{:S(2)}) collective-permute-start(bf16[192,1536]{1,0:T(8,128)(2,1)S(1)} %get-tuple-element.64), channel_id=1, source_target_pairs={{0,24},{8,0},{16,8},{24,16},{1,25},{9,1},{17,9},{25,17},{2,26},{10... | collective-permute-start | bytes 1769480 | tf_op jit(solution)/shard_map/ppermute | solution.py:27
  127.0 9.9 %collective-permute-start.15 = (bf16[192,1536]{1,0:T(8,128)(2,1)S(1)}, bf16[192,1536]{1,0:T(8,128)(2,1)S(1)}, u32[]{:S(2)}, u32[]{:S(2)}) collective-permute-start(bf16[192,1536]{1,0:T(8,128)(2,1)S(1)} %add_convert_fusion.3), channel_id=1, source_target_pairs={{0,32},{32,64},{64,96},{96,0},{1,33},{33,65},{65,97},{97,1},{2,34}... | collective-permute-start | bytes 1769480 | tf_op jit(solution)/shard_map/ppermute | solution.py:27
  127.9 17.0 %collective-permute-start.19 = (bf16[192,1536]{1,0:T(8,128)(2,1)S(1)}, bf16[192,1536]{1,0:T(8,128)(2,1)S(1)}, u32[]{:S(2)}, u32[]{:S(2)}) collective-permute-start(bf16[192,1536]{1,0:T(8,128)(2,1)S(1)} %add_convert_fusion.2), channel_id=1, source_target_pairs={{0,96},{32,0},{64,32},{96,64},{1,97},{33,1},{65,33},{97,65},{2,98}... | collective-permute-start | bytes 1769480 | tf_op jit(solution)/shard_map/ppermute | solution.py:27
  131.6 29.0 %collective-permute-start.27 = (bf16[192,1536]{1,0:T(8,128)(2,1)S(1)}, bf16[192,1536]{1,0:T(8,128)(2,1)S(1)}, u32[]{:S(2)}, u32[]{:S(2)}) collective-permute-start(bf16[192,1536]{1,0:T(8,128)(2,1)S(1)} %get-tuple-element.65), channel_id=1, source_target_pairs={{0,8},{8,16},{16,24},{24,0},{1,9},{9,17},{17,25},{25,1},{2,10},{10... | collective-permute-start | bytes 1769480 | tf_op jit(solution)/shard_map/ppermute | solution.py:27
  131.6 29.0 %collective-permute-start.25 = (bf16[192,1536]{1,0:T(8,128)(2,1)}, bf16[192,1536]{1,0:T(8,128)(2,1)S(1)}, u32[]{:S(2)}, u32[]{:S(2)}) collective-permute-start(bf16[192,1536]{1,0:T(8,128)(2,1)} %add_convert_fusion.1), channel_id=1, source_target_pairs={{0,8},{8,16},{16,24},{24,0},{1,9},{9,17},{17,25},{25,1},{2,10},{10... | collective-permute-start | bytes 1769480 | tf_op jit(solution)/shard_map/ppermute | solution.py:27
  136.9 24.5 %collective-permute-start.29 = (bf16[192,1536]{1,0:T(8,128)(2,1)}, bf16[192,1536]{1,0:T(8,128)(2,1)}, u32[]{:S(2)}, u32[]{:S(2)}) collective-permute-start(bf16[192,1536]{1,0:T(8,128)(2,1)} %add_convert_fusion), channel_id=1, source_target_pairs={{0,24},{8,0},{16,8},{24,16},{1,25},{9,1},{17,9},{25,17},{2,26},{10... | collective-permute-start | bytes 1769480 | tf_op jit(solution)/shard_map/ppermute | solution.py:27
  146.9 23.4 %all-to-all-start = ((f32[128,1,128]{2,1,0:T(1,128)}), f32[128,1,128]{2,1,0:T(1,128)S(1)}, u32[]{:S(2)}, u32[]{:S(2)}) async-start(f32[128,1,128]{2,1,0:T(1,128)} %bitcast.6), calls=%async_computation | async-start | bytes 131072 | tf_op jit(solution)/shard_map/all_to_all | solution.py:450
  178.6 8.7 %all-to-all-start.1 = ((f32[8,1,384]{2,1,0:T(1,128)}), f32[8,1,384]{2,1,0:T(1,128)S(1)}, u32[]{:S(2)}, u32[]{:S(2)}) async-start(f32[8,1,384]{2,1,0:T(1,128)} %get-tuple-element.59), calls=%async_computation.1 | async-start | bytes 24576 | tf_op jit(solution)/shard_map/all_to_all | solution.py:458
  (5 other events, 91.8 us)

commit v2 on v1

--- a/solution.py
+++ b/solution.py
@@ -273,7 +273,7 @@
             pl.BlockSpec((S, C), lambda i: (0, 0)),
             pl.BlockSpec((128, 128), lambda i: (0, 0)),
         ],
-        out_shape=[pltpu.HBM((S, C), F32), pltpu.HBM((128, 128), F32)],
+        out_shape=[pltpu.HBM((S, C), F32), jax.ShapeDtypeStruct((128, 128), F32)],
         compiler_params=params(24),
         name="fold_grad",
     )(*args)
@@ -337,8 +337,8 @@
         right = jnp.concatenate([w[:, at] for w in weights], axis=0)
         for k in range(count):
             total = jnp.dot(rows[k][0], right, preferred_element_type=F32)
-            if own_last:
-                outs[k][:, at] = total
+            if own_last or count == 2:
+                outs[k][:, at] = total.astype(outs[k].dtype)
             else:
                 outs[2 * k][:, at] = total[:HALF].astype(BF)
                 outs[2 * k + 1][:, at] = total[HALF:].astype(BF)
@@ -350,6 +350,8 @@
 def input_grad(rows, blocks, weights, own):
     half = jax.ShapeDtypeStruct((HALF, C), BF)
     outs = [pltpu.HBM((S, C), F32)] if own else [half] * (2 * len(blocks))
+    if len(blocks) == 2:
+        outs = [jax.ShapeDtypeStruct((S, C), BF)] * 2
 
     def piece(k):
         return pl.BlockSpec((1, S, C), lambda i: (k, 0, 0))
@@ -413,6 +415,17 @@
     return left_a, left_b, right_a, right_b
 
 
+def ring_scatter_whole(far, near, axis):
+    up, down = near
+    from_left = shift(far[0], axis, 1)
+    from_right = shift(far[1], axis, -1)
+    up_a = (up[:HALF].astype(F32) + from_left.astype(F32)).astype(BF)
+    down_b = (down[HALF:].astype(F32) + from_right.astype(F32)).astype(BF)
+    up = lax.dynamic_update_slice(up, up_a, (0, 0))
+    down = lax.dynamic_update_slice(down, down_b, (HALF, 0))
+    return shift(up, axis, 1), shift(down, axis, -1)
+
+
 CHUNKS = ((0, C),)
 
 
@@ -442,10 +455,9 @@
     i_far = input_grad(rows, (3,), weights, False)
     i_near = input_grad(rows, (2, 1), weights, False)
     (i_own,) = input_grad(rows, (0,), weights, True)
-    left_a, left_b, right_a, right_b = ring_scatter(i_far, i_near, "x")
-    top = i_own[:HALF] + left_a.astype(F32) + right_a.astype(F32)
-    bottom = i_own[HALF:] + left_b.astype(F32) + right_b.astype(F32)
-    grad_input = jnp.concatenate([top, bottom], axis=0).astype(BF)
+    left, right = ring_scatter_whole(i_far, i_near, "x")
+    peaks, i_own = lax.optimization_barrier((peaks, i_own))
+    grad_input = (i_own + left.astype(F32) + right.astype(F32)).astype(BF)
     gradient, pair = fold_grad(parts, CHUNKS, peaks)
     pairs = lax.all_to_all(pair, ALL, 0, 0, tiled=True)
     gradient, moment, second, master = (

time: 189 us -> 181 us (0.958)
  blocking collectives: 0 us -> 20.4 us
  starting transfers between devices: 62.8 us -> 44.1 us
  waiting for transfers between devices: 76.3 us -> 67.5 us
    all_to_all x0 -> x1, blocking collectives: none -> 20.4 us  [step(): pairs = lax.all_to_all(pair, ALL, 0, 0, tiled=True)]
    all_to_all x1 -> x0, starting transfers between devices: 13.7 us -> none  [step(): pairs = lax.all_to_all(pair, ALL, 0, 0, tiled=True)]
    all_to_all x1 -> x0, waiting for transfers between devices: 5.63 us -> none  [step(): pairs = lax.all_to_all(pair, ALL, 0, 0, tiled=True)]
    ppermute x30 -> x28, starting transfers between devices: 45.1 us -> 40.1 us  [shift(): return lax.ppermute(v, axis, [(i, (i + by) % n) for i in range(n)])]
    convert_element_type x0 -> x1, other arithmetic: none -> 3.8 us  [step(): grad_input = (i_own + left.astype(F32) + right.astype(F32)).astype(BF)]
    another operation x1 -> x0, other arithmetic: 3.22 us -> none
    dynamic_update_slice x0 -> x2, other arithmetic: none -> 2.22 us  [the longest x1 2.02 us: ring_scatter_whole(): down = lax.dynamic_update_slice(down, down_b, (HALF, 0))]
    concatenate x1 -> x0, other arithmetic: 2.15 us -> none  [step(): grad_input = jnp.concatenate([top, bottom], axis=0).astype(BF)]
  transfers between devices with their start and end apart: 32 -> 29, of which waited for: 11 -> 11; matrix products, arithmetic and copies ran while one was open for 5% -> 4% of each run, Pallas kernels for 15% -> 19%
where the time goes in v2:
time: 181 us
  waiting for transfers between devices  67.5 us (37%)
  starting transfers between devices  44.1 us (24%)
  Pallas kernels  40.2 us (22%)
  blocking collectives  20.4 us (11%)
  other arithmetic  7.18 us (4%)
    ppermute x28, waiting for transfers between devices, shift(): return lax.ppermute(v, axis, [(i, (i + by) % n) for i in range(n)])  66.6 us
    ppermute x28, starting transfers between devices, shift(): return lax.ppermute(v, axis, [(i, (i + by) % n) for i in range(n)])  40.1 us
    all_to_all x1, blocking collectives, step(): pairs = lax.all_to_all(pair, ALL, 0, 0, tiled=True)  20.4 us
    pallas_call x3, Pallas kernels, input_grad(): pl.pallas_call(functools.partial(input_grad_kernel, len(blocks), own), gr...  12.9 us
    pallas_call x1, Pallas kernels, weight_grad(): pl.pallas_call(functools.partial(weight_grad_kernel, blocks, width), grid...  8.42 us
    pallas_call x1, Pallas kernels, adam(): pl.pallas_call(adam_kernel, grid=(S // ROWS,), in_specs=[pl.BlockSpec((12...  8.34 us
    all_to_all x1, starting transfers between devices, step(): highs = lax.all_to_all(high, TENSOR, 0, 0, tiled=True)  4 us
    convert_element_type x1, other arithmetic, step(): grad_input = (i_own + left.astype(F32) + right.astype(F32)).astype(BF)  3.8 us
  transfers between devices with their start and end apart: 29, of which 11 were waited for; matrix products, arithmetic and copies ran while one was open for 4% of the time, Pallas kernels for 19%

profile of v2, /device:TPU:1, one launch (start us, length us, event | category | flops | bytes accessed | tf_op | source)
XLA Modules:
  0.0 181.1 jit_solution(13609162562361428369)
XLA Ops:
  2.0 2.1 %collective-permute-start = (bf16[48,1536]{1,0:T(8,128)(2,1)S(1)}, bf16[48,1536]{1,0:T(8,128)(2,1)S(1)}, u32[]{:S(2)}, u32[]{:S(2)}) collective-permute-start(bf16[48,1536]{1,0:T(8,128)(2,1)S(1)} %get-tuple-element.43), channel_id=1, source_target_pairs={{0,8},{8,16},{16,24},{24,0},{1,9},{9,17},{17,25},{25,1},{2,10},{10... | collective-permute-start | bytes 442376 | tf_op jit(solution)/shard_map/ppermute | solution.py:27
  5.7 3.9 %collective-permute-start.22 = (bf16[384,1536]{1,0:T(8,128)(2,1)S(1)}, bf16[384,1536]{1,0:T(8,128)(2,1)S(1)}, u32[]{:S(2)}, u32[]{:S(2)}) collective-permute-start(bf16[384,1536]{1,0:T(8,128)(2,1)S(1)} %multiply_convert_fusion.refs_5_.refs_6_), channel_id=1, source_target_pairs={{0,96},{32,0},{64,32},{96,64},{1,97},{33,1},{65,33},{97,65},{2,98}... | collective-permute-start | bytes 3538952 | tf_op jit(solution)/shard_map/ppermute | solution.py:27
  9.7 2.7 %collective-permute-start.1 = (bf16[48,1536]{1,0:T(8,128)(2,1)S(1)}, bf16[48,1536]{1,0:T(8,128)(2,1)S(1)}, u32[]{:S(2)}, u32[]{:S(2)}) collective-permute-start(bf16[48,1536]{1,0:T(8,128)(2,1)S(1)} %get-tuple-element.44), channel_id=1, source_target_pairs={{0,24},{8,0},{16,8},{24,16},{1,25},{9,1},{17,9},{25,17},{2,26},{10... | collective-permute-start | bytes 442376 | tf_op jit(solution)/shard_map/ppermute | solution.py:27
  12.3 21.5 %collective-permute-done.1 = bf16[48,1536]{1,0:T(8,128)(2,1)S(1)} collective-permute-done((bf16[48,1536]{1,0:T(8,128)(2,1)S(1)}, bf16[48,1536]{1,0:T(8,128)(2,1)S(1)}, u32[]{:S(2)}, u32[]{:S(2)}) %collective-permute-start.1) | collective-permute-done | bytes 147488 | tf_op jit(solution)/shard_map/ppermute | solution.py:27
  33.8 2.5 %collective-permute-start.2 = (bf16[48,1536]{1,0:T(8,128)(2,1)S(1)}, bf16[48,1536]{1,0:T(8,128)(2,1)S(1)}, u32[]{:S(2)}, u32[]{:S(2)}) collective-permute-start(bf16[48,1536]{1,0:T(8,128)(2,1)S(1)} %get-tuple-element.45), channel_id=1, source_target_pairs={{0,16},{8,24},{16,0},{24,8},{1,17},{9,25},{17,1},{25,9},{2,18},{10... | collective-permute-start | bytes 442376 | tf_op jit(solution)/shard_map/ppermute | solution.py:27
  36.3 3.7 %collective-permute-done.2 = bf16[48,1536]{1,0:T(8,128)(2,1)S(1)} collective-permute-done((bf16[48,1536]{1,0:T(8,128)(2,1)S(1)}, bf16[48,1536]{1,0:T(8,128)(2,1)S(1)}, u32[]{:S(2)}, u32[]{:S(2)}) %collective-permute-start.2) | collective-permute-done | bytes 147488 | tf_op jit(solution)/shard_map/ppermute | solution.py:27
  40.0 2.3 %collective-permute-start.6 = (bf16[144,1536]{1,0:T(8,128)(2,1)S(1)}, bf16[144,1536]{1,0:T(8,128)(2,1)S(1)}, u32[]{:S(2)}, u32[]{:S(2)}) collective-permute-start(bf16[144,1536]{1,0:T(8,128)(2,1)S(1)} %constant_dynamic-update-slice_fusion.refs_1_), channel_id=1, source_target_pairs={{0,1},{1,0},{2,3},{3,2},{4,5},{5,4},{6,7},{7,6},{8,9},{9,8},{10,11... | collective-permute-start | bytes 1327112 | tf_op jit(solution)/shard_map/ppermute | solution.py:27
  43.8 2.9 %collective-permute-start.5 = (bf16[144,1536]{1,0:T(8,128)(2,1)S(1)}, bf16[144,1536]{1,0:T(8,128)(2,1)S(1)}, u32[]{:S(2)}, u32[]{:S(2)}) collective-permute-start(bf16[144,1536]{1,0:T(8,128)(2,1)S(1)} %constant_dynamic-update-slice_fusion.refs_1_), channel_id=1, source_target_pairs={{0,4},{2,6},{4,0},{6,2},{1,5},{3,7},{5,1},{7,3},{8,12},{10,14},{12... | collective-permute-start | bytes 1327112 | tf_op jit(solution)/shard_map/ppermute | solution.py:27
  48.3 8.4 %collective-permute-done.5.refs_4_ = bf16[144,1536]{1,0:T(8,128)(2,1)S(1)} collective-permute-done((bf16[144,1536]{1,0:T(8,128)(2,1)S(1)}, bf16[144,1536]{1,0:T(8,128)(2,1)S(1)}, u32[]{:S(2)}, u32[]{:S(2)}) %collective-permute-start.5) | collective-permute-done | bytes 442400 | tf_op jit(solution)/shard_map/ppermute | solution.py:27
  56.7 2.7 %collective-permute-start.13 = (bf16[192,1536]{1,0:T(8,128)(2,1)S(1)}, bf16[192,1536]{1,0:T(8,128)(2,1)S(1)}, u32[]{:S(2)}, u32[]{:S(2)}) collective-permute-start(bf16[192,1536]{1,0:T(8,128)(2,1)S(1)} %slice.29), channel_id=1, source_target_pairs={{0,24},{8,0},{16,8},{24,16},{1,25},{9,1},{17,9},{25,17},{2,26},{10... | collective-permute-start | bytes 1769480 | tf_op jit(solution)/shard_map/ppermute | solution.py:27
  59.4 7.2 %collective-permute-done.4.refs_3_ = bf16[144,1536]{1,0:T(8,128)(2,1)S(1)} collective-permute-done((bf16[144,1536]{1,0:T(8,128)(2,1)S(1)}, bf16[144,1536]{1,0:T(8,128)(2,1)S(1)}, u32[]{:S(2)}, u32[]{:S(2)}) %collective-permute-start.4) | collective-permute-done | bytes 442400 | tf_op jit(solution)/shard_map/ppermute | solution.py:27
  70.6 3.8 %collective-permute-start.23 = (bf16[192,1536]{1,0:T(8,128)(2,1)S(1)}, bf16[192,1536]{1,0:T(8,128)(2,1)S(1)}, u32[]{:S(2)}, u32[]{:S(2)}) collective-permute-start(bf16[192,1536]{1,0:T(8,128)(2,1)S(1)} %slice.31), channel_id=1, source_target_pairs={{0,96},{32,0},{64,32},{96,64},{1,97},{33,1},{65,33},{97,65},{2,98}... | collective-permute-start | bytes 1769480 | tf_op jit(solution)/shard_map/ppermute | solution.py:27
  74.4 1.6 assemble_grads.1
  76.1 5.3 %collective-permute-done.12.refs_6_.top_ref = bf16[192,1536]{1,0:T(8,128)(2,1)S(1)} collective-permute-done((bf16[192,1536]{1,0:T(8,128)(2,1)S(1)}, bf16[192,1536]{1,0:T(8,128)(2,1)S(1)}, u32[]{:S(2)}, u32[]{:S(2)}) %collective-permute-start.12) | collective-permute-done | bytes 589856 | tf_op jit(solution)/shard_map/ppermute | solution.py:27
  81.4 8.4 %weight_grad.1 = (bf16[192,1536]{1,0:T(8,128)(2,1)S(1)}, bf16[192,1536]{1,0:T(8,128)(2,1)S(1)}, bf16[192,1536]{1,0:T(8,128)(2,1)S(1)}, bf16[192,1536]{1,0:T(8,12...) custom-call(bf16[4,384,1536]{2,1,0:T(8,128)(2,1)S(1)} %get-tuple-element.46.refs_0_.refs_1_.refs_2_.cols_ref, ...), custom_call_target="tpu_custom_call" | custom-call | flops 5435817984 | bytes 9437184 | tf_op jit(solution)/shard_map/weight_grad/pallas_call | solution.py:143
  89.9 2.9 %input_grad.5 = (bf16[192,1536]{1,0:T(8,128)(2,1)S(1)}, bf16[192,1536]{1,0:T(8,128)(2,1)S(1)}) custom-call(bf16[4,384,1536]{2,1,0:T(8,128)(2,1)S(1)} %get-tuple-element.59.refs_0_.refs_1_, bf16[192,1536]{1,0:T(8,128)(2,1)S(1)} %collective-permute-done.21.refs_1_.refs_2_, bf16[192,1536]{1,0:T(8,128)(2,1)S(1)} %collective-permute-done.23.refs_2_.refs_3_, ...), custom_call_target="tpu_custom_call" | custom-call | flops 1811939328 | bytes 9437184 | tf_op jit(solution)/shard_map/input_grad/pallas_call | solution.py:362
  94.3 2.8 %far_start.1 = (f32[384,1536]{1,0:T(8,128)S(1)}, f32[8,256]{1,0:T(8,128)S(1)}) custom-call(bf16[4,384,1536]{2,1,0:T(8,128)(2,1)S(1)} %get-tuple-element.46.refs_0_.refs_1_.refs_2_.cols_ref, bf16[384,1536]{1,0:T(8,128)(2,1)S(1)} %copy-done, bf16[384,1536]{1,0:T(8,128)(2,1)S(1)} %collective-permute-done.10.refs_4_.left_ref, ...), custom_call_target="tpu_custom_call" | custom-call | flops 1358954496 | bytes 6291456 | tf_op jit(solution)/shard_map/far_start/pallas_call | solution.py:200
  97.1 1.6 far_finish.1
  98.7 1.7 collective-permute-start.14
  100.4 2.2 %collective-permute-start.18 = (bf16[192,1536]{1,0:T(8,128)(2,1)S(1)}, bf16[192,1536]{1,0:T(8,128)(2,1)S(1)}, u32[]{:S(2)}, u32[]{:S(2)}) collective-permute-start(bf16[192,1536]{1,0:T(8,128)(2,1)S(1)} %get-tuple-element.55), channel_id=1, source_target_pairs={{0,96},{32,0},{64,32},{96,64},{1,97},{33,1},{65,33},{97,65},{2,98}... | collective-permute-start | bytes 1769480 | tf_op jit(solution)/shard_map/ppermute | solution.py:27
  102.6 5.7 %input_grad.4 = (bf16[384,1536]{1,0:T(8,128)(2,1)S(1)}, bf16[384,1536]{1,0:T(8,128)(2,1)}) custom-call(bf16[4,384,1536]{2,1,0:T(8,128)(2,1)S(1)} %get-tuple-element.59.refs_0_.refs_1_, bf16[4,384,1536]{2,1,0:T(8,128)(2,1)S(1)} %get-tuple-element.59.refs_0_.refs_1_, bf16[192,1536]{1,0:T(8,128)(2,1)S(1)} %collective-permute-done.21.refs_1_.refs_2_, ...), custom_call_target="tpu_custom_call" | custom-call | flops 3623878656 | bytes 9437184 | tf_op jit(solution)/shard_map/input_grad/pallas_call | solution.py:362
  108.3 2.7 %collective-permute-start.17 = (bf16[192,1536]{1,0:T(8,128)(2,1)S(1)}, bf16[192,1536]{1,0:T(8,128)(2,1)S(1)}, u32[]{:S(2)}, u32[]{:S(2)}) collective-permute-start(bf16[192,1536]{1,0:T(8,128)(2,1)S(1)} %get-tuple-element.53), channel_id=1, source_target_pairs={{0,96},{32,0},{64,32},{96,64},{1,97},{33,1},{65,33},{97,65},{2,98}... | collective-permute-start | bytes 1769480 | tf_op jit(solution)/shard_map/ppermute | solution.py:27
  111.0 2.0 %fusion.1 = bf16[384,1536]{1,0:T(8,128)(2,1)} fusion(bf16[384,1536]{1,0:T(8,128)(2,1)} %get-tuple-element.68, bf16[192,1536]{1,0:T(8,128)(2,1)S(1)} %collective-permute-done.26), kind=kLoop, calls=%fused_computation.7 | loop fusion | flops 1179648 | bytes 1769472 | tf_op jit(solution)/shard_map/dynamic_update_slice | solution.py:425
  113.0 3.1 %collective-permute-done.24 = bf16[192,1536]{1,0:T(8,128)(2,1)S(1)} collective-permute-done((bf16[192,1536]{1,0:T(8,128)(2,1)S(1)}, bf16[192,1536]{1,0:T(8,128)(2,1)S(1)}, u32[]{:S(2)}, u32[]{:S(2)}) %collective-permute-start.24) | collective-permute-done | bytes 589856 | tf_op jit(solution)/shard_map/ppermute | solution.py:27
  118.6 8.1 %collective-permute-done.16.refs_2_ = bf16[192,1536]{1,0:T(8,128)(2,1)S(1)} collective-permute-done((bf16[192,1536]{1,0:T(8,128)(2,1)S(1)}, bf16[192,1536]{1,0:T(8,128)(2,1)S(1)}, u32[]{:S(2)}, u32[]{:S(2)}) %collective-permute-start.16) | collective-permute-done | bytes 589856 | tf_op jit(solution)/shard_map/ppermute | solution.py:27
  127.8 4.3 %input_grad.3 = f32[384,1536]{1,0:T(8,128)} custom-call(bf16[4,384,1536]{2,1,0:T(8,128)(2,1)S(1)} %get-tuple-element.59.refs_0_.refs_1_, bf16[192,1536]{1,0:T(8,128)(2,1)S(1)} %collective-permute-done.21.refs_1_.refs_2_, bf16[192,1536]{1,0:T(8,128)(2,1)S(1)} %collective-permute-done.23.refs_2_.refs_3_, ...), custom_call_target="tpu_custom_call" | custom-call | flops 1811939328 | bytes 9437184 | tf_op jit(solution)/shard_map/input_grad/pallas_call | solution.py:362
  132.1 7.1 %collective-permute-done.15.refs_1_ = bf16[192,1536]{1,0:T(8,128)(2,1)S(1)} collective-permute-done((bf16[192,1536]{1,0:T(8,128)(2,1)S(1)}, bf16[192,1536]{1,0:T(8,128)(2,1)S(1)}, u32[]{:S(2)}, u32[]{:S(2)}) %collective-permute-start.15) | collective-permute-done | bytes 589856 | tf_op jit(solution)/shard_map/ppermute | solution.py:27
  139.2 2.0 %fold_grad.1 = (f32[384,1536]{1,0:T(8,128)}, f32[128,128]{1,0:T(8,128)S(1)}) custom-call(f32[384,1536]{1,0:T(8,128)S(1)} %get-tuple-element.47.refs_0_, bf16[192,1536]{1,0:T(8,128)(2,1)S(1)} %collective-permute-done.15.refs_1_, bf16[192,1536]{1,0:T(8,128)(2,1)S(1)} %collective-permute-done.16.refs_2_, bf16[192,1536]{1,0:T(8,128)(2,1)S(1)} %collective-permute-done.17.refs_3_, ...), custom_call_target="tpu_custom_call" | custom-call | tf_op jit(solution)/shard_map/fold_grad/pallas_call | solution.py:268
  141.2 20.4 %all_to_all.16 = f32[128,1,128]{2,1,0:T(1,128)S(1)} all-to-all(f32[128,1,128]{2,1,0:T(1,128)S(1)} %bitcast.8), channel_id=1, replica_groups=mesh['z'=4,'x'=4,'y'=4,'c'=2] {'z','x','y','c'}, dimensions={0} | all-to-all | bytes 131072 | tf_op jit(solution)/shard_map/all_to_all | solution.py:462
  161.6 8.3 %adam.1 = (f32[384,1536]{1,0:T(8,128)}, f32[384,1536]{1,0:T(8,128)}, f32[384,1536]{1,0:T(8,128)}, f32[8,1,384]{2,1,0:T(1,128)S(1)}, f32[8,128]{1,0:T(8,128)S(1)}, /*index=5*/f32[384,1536]{1,0:T(8,128)S(1)}) custom-call(f32[128,128]{1,0:T(8,128)S(1)} %bitcast.7, f32[384,1536]{1,0:T(8,128)} %get-tuple-element.63.grad_ref, f32[384,1536]{1,0:T(8,128)} %moment_ref.1, ...), custom_call_target="tpu_custom_call" | custom-call | tf_op jit(solution)/shard_map/adam/pallas_call | solution.py:318
  170.5 4.0 %all-to-all-start.1 = ((f32[8,1,384]{2,1,0:T(1,128)}), f32[8,1,384]{2,1,0:T(1,128)S(1)}, u32[]{:S(2)}, u32[]{:S(2)}) async-start(f32[8,1,384]{2,1,0:T(1,128)} %copy-done.1), calls=%async_computation.1 | async-start | bytes 24576 | tf_op jit(solution)/shard_map/all_to_all | solution.py:470
  174.5 3.8 %add_convert_fusion = bf16[384,1536]{1,0:T(8,128)(2,1)} fusion(bf16[384,1536]{1,0:T(8,128)(2,1)} %collective-permute-done.27, f32[384,1536]{1,0:T(8,128)} %input_grad.3, bf16[384,1536]{1,0:T(8,128)(2,1)} %collective-permute-done.25), kind=kLoop, calls=%fused_computation | loop fusion | flops 2949120 | bytes 5898240 | tf_op jit(solution)/shard_map/convert_element_type | solution.py:460
  (67 shorter events, 18.6 us)
Async XLA Ops:
  0.6 4.8 %copy-start.3 = (bf16[384]{0:T(512)(128)(2,1)S(1)}, bf16[384]{0:T(512)(128)(2,1)}, u32[]{:S(2)}) copy-start(bf16[384]{0:T(512)(128)(2,1)} %param.10) | copy-start | bytes 2308
  0.7 73.8 %slice-start = ((s8[4718592]{0:T(1024)(128)(4,1)}), s8[4194304]{0:T(1024)(128)(4,1)S(1)}, s32[]{:S(2)}) async-start(s8[4718592]{0:T(1024)(128)(4,1)} %bitcast.5), calls=%async_computation.2 | async-start | bytes 8388608
  2.0 7.7 %collective-permute-start = (bf16[48,1536]{1,0:T(8,128)(2,1)S(1)}, bf16[48,1536]{1,0:T(8,128)(2,1)S(1)}, u32[]{:S(2)}, u32[]{:S(2)}) collective-permute-start(bf16[48,1536]{1,0:T(8,128)(2,1)S(1)} %get-tuple-element.43), channel_id=1, source_target_pairs={{0,8},{8,16},{16,24},{24,0},{1,9},{9,17},{17,25},{25,1},{2,10},{10... | collective-permute-start | bytes 442376 | tf_op jit(solution)/shard_map/ppermute | solution.py:27
  4.1 42.6 %collective-permute-start.11 = (bf16[384,1536]{1,0:T(8,128)(2,1)S(1)}, bf16[384,1536]{1,0:T(8,128)(2,1)S(1)}, u32[]{:S(2)}, u32[]{:S(2)}) collective-permute-start(bf16[384,1536]{1,0:T(8,128)(2,1)S(1)} %copy-done), channel_id=1, source_target_pairs={{0,24},{8,0},{16,8},{24,16},{1,25},{9,1},{17,9},{25,17},{2,26},{10... | collective-permute-start | bytes 3538952 | tf_op jit(solution)/shard_map/ppermute | solution.py:27
  5.4 69.0 %slice-start.1 = ((s8[4718592]{0:T(1024)(128)(4,1)}), s8[524288]{0:T(1024)(128)(4,1)S(1)}, s32[]{:S(2)}) async-start(s8[4718592]{0:T(1024)(128)(4,1)} %bitcast.5), calls=%async_computation.3 | async-start | bytes 1048576
  5.7 63.5 %collective-permute-start.22 = (bf16[384,1536]{1,0:T(8,128)(2,1)S(1)}, bf16[384,1536]{1,0:T(8,128)(2,1)S(1)}, u32[]{:S(2)}, u32[]{:S(2)}) collective-permute-start(bf16[384,1536]{1,0:T(8,128)(2,1)S(1)} %multiply_convert_fusion.refs_5_.refs_6_), channel_id=1, source_target_pairs={{0,96},{32,0},{64,32},{96,64},{1,97},{33,1},{65,33},{97,65},{2,98}... | collective-permute-start | bytes 3538952 | tf_op jit(solution)/shard_map/ppermute | solution.py:27
  9.6 59.7 %collective-permute-start.20 = (bf16[384,1536]{1,0:T(8,128)(2,1)S(1)}, bf16[384,1536]{1,0:T(8,128)(2,1)S(1)}, u32[]{:S(2)}, u32[]{:S(2)}) collective-permute-start(bf16[384,1536]{1,0:T(8,128)(2,1)S(1)} %multiply_convert_fusion.refs_5_.refs_6_), channel_id=1, source_target_pairs={{0,32},{32,64},{64,96},{96,0},{1,33},{33,65},{65,97},{97,1},{2,34}... | collective-permute-start | bytes 3538952 | tf_op jit(solution)/shard_map/ppermute | solution.py:27
  9.6 37.8 %collective-permute-start.10 = (bf16[384,1536]{1,0:T(8,128)(2,1)S(1)}, bf16[384,1536]{1,0:T(8,128)(2,1)S(1)}, u32[]{:S(2)}, u32[]{:S(2)}) collective-permute-start(bf16[384,1536]{1,0:T(8,128)(2,1)S(1)} %copy-done), channel_id=1, source_target_pairs={{0,8},{8,16},{16,24},{24,0},{1,9},{9,17},{17,25},{25,1},{2,10},{10... | collective-permute-start | bytes 3538952 | tf_op jit(solution)/shard_map/ppermute | solution.py:27
  9.7 24.1 %collective-permute-start.1 = (bf16[48,1536]{1,0:T(8,128)(2,1)S(1)}, bf16[48,1536]{1,0:T(8,128)(2,1)S(1)}, u32[]{:S(2)}, u32[]{:S(2)}) collective-permute-start(bf16[48,1536]{1,0:T(8,128)(2,1)S(1)} %get-tuple-element.44), channel_id=1, source_target_pairs={{0,24},{8,0},{16,8},{24,16},{1,25},{9,1},{17,9},{25,17},{2,26},{10... | collective-permute-start | bytes 442376 | tf_op jit(solution)/shard_map/ppermute | solution.py:27
  33.8 6.2 %collective-permute-start.2 = (bf16[48,1536]{1,0:T(8,128)(2,1)S(1)}, bf16[48,1536]{1,0:T(8,128)(2,1)S(1)}, u32[]{:S(2)}, u32[]{:S(2)}) collective-permute-start(bf16[48,1536]{1,0:T(8,128)(2,1)S(1)} %get-tuple-element.45), channel_id=1, source_target_pairs={{0,16},{8,24},{16,0},{24,8},{1,17},{9,25},{17,1},{25,9},{2,18},{10... | collective-permute-start | bytes 442376 | tf_op jit(solution)/shard_map/ppermute | solution.py:27
  40.0 3.8 %collective-permute-start.6 = (bf16[144,1536]{1,0:T(8,128)(2,1)S(1)}, bf16[144,1536]{1,0:T(8,128)(2,1)S(1)}, u32[]{:S(2)}, u32[]{:S(2)}) collective-permute-start(bf16[144,1536]{1,0:T(8,128)(2,1)S(1)} %constant_dynamic-update-slice_fusion.refs_1_), channel_id=1, source_target_pairs={{0,1},{1,0},{2,3},{3,2},{4,5},{5,4},{6,7},{7,6},{8,9},{9,8},{10,11... | collective-permute-start | bytes 1327112 | tf_op jit(solution)/shard_map/ppermute | solution.py:27
  43.8 12.9 %collective-permute-start.5 = (bf16[144,1536]{1,0:T(8,128)(2,1)S(1)}, bf16[144,1536]{1,0:T(8,128)(2,1)S(1)}, u32[]{:S(2)}, u32[]{:S(2)}) collective-permute-start(bf16[144,1536]{1,0:T(8,128)(2,1)S(1)} %constant_dynamic-update-slice_fusion.refs_1_), channel_id=1, source_target_pairs={{0,4},{2,6},{4,0},{6,2},{1,5},{3,7},{5,1},{7,3},{8,12},{10,14},{12... | collective-permute-start | bytes 1327112 | tf_op jit(solution)/shard_map/ppermute | solution.py:27
  46.7 19.8 %collective-permute-start.4 = (bf16[144,1536]{1,0:T(8,128)(2,1)S(1)}, bf16[144,1536]{1,0:T(8,128)(2,1)S(1)}, u32[]{:S(2)}, u32[]{:S(2)}) collective-permute-start(bf16[144,1536]{1,0:T(8,128)(2,1)S(1)} %constant_dynamic-update-slice_fusion.refs_1_), channel_id=1, source_target_pairs={{0,6},{2,0},{4,2},{6,4},{1,7},{3,1},{5,3},{7,5},{8,14},{10,8},{12,... | collective-permute-start | bytes 1327112 | tf_op jit(solution)/shard_map/ppermute | solution.py:27
  47.5 20.2 %collective-permute-start.3 = (bf16[144,1536]{1,0:T(8,128)(2,1)S(1)}, bf16[144,1536]{1,0:T(8,128)(2,1)S(1)}, u32[]{:S(2)}, u32[]{:S(2)}) collective-permute-start(bf16[144,1536]{1,0:T(8,128)(2,1)S(1)} %constant_dynamic-update-slice_fusion.refs_1_), channel_id=1, source_target_pairs={{0,2},{2,4},{4,6},{6,0},{1,3},{3,5},{5,7},{7,1},{8,10},{10,12},{12... | collective-permute-start | bytes 1327112 | tf_op jit(solution)/shard_map/ppermute | solution.py:27
  56.7 19.4 %collective-permute-start.13 = (bf16[192,1536]{1,0:T(8,128)(2,1)S(1)}, bf16[192,1536]{1,0:T(8,128)(2,1)S(1)}, u32[]{:S(2)}, u32[]{:S(2)}) collective-permute-start(bf16[192,1536]{1,0:T(8,128)(2,1)S(1)} %slice.29), channel_id=1, source_target_pairs={{0,24},{8,0},{16,8},{24,16},{1,25},{9,1},{17,9},{25,17},{2,26},{10... | collective-permute-start | bytes 1769480 | tf_op jit(solution)/shard_map/ppermute | solution.py:27
  66.5 14.9 %collective-permute-start.12 = (bf16[192,1536]{1,0:T(8,128)(2,1)S(1)}, bf16[192,1536]{1,0:T(8,128)(2,1)S(1)}, u32[]{:S(2)}, u32[]{:S(2)}) collective-permute-start(bf16[192,1536]{1,0:T(8,128)(2,1)S(1)} %slice.28), channel_id=1, source_target_pairs={{0,8},{8,16},{16,24},{24,0},{1,9},{9,17},{17,25},{25,1},{2,10},{10... | collective-permute-start | bytes 1769480 | tf_op jit(solution)/shard_map/ppermute | solution.py:27
  67.7 2.9 %collective-permute-start.9 = (bf16[144,1536]{1,0:T(8,128)(2,1)S(1)}, bf16[144,1536]{1,0:T(8,128)(2,1)S(1)}, u32[]{:S(2)}, u32[]{:S(2)}) collective-permute-start(bf16[144,1536]{1,0:T(8,128)(2,1)S(1)} %collective-permute-done.5.refs_4_), channel_id=1, source_target_pairs={{0,1},{1,0},{2,3},{3,2},{4,5},{5,4},{6,7},{7,6},{8,9},{9,8},{10,11... | collective-permute-start | bytes 1327112 | tf_op jit(solution)/shard_map/ppermute | solution.py:27
  69.2 5.2 %collective-permute-start.8 = (bf16[144,1536]{1,0:T(8,128)(2,1)S(1)}, bf16[144,1536]{1,0:T(8,128)(2,1)S(1)}, u32[]{:S(2)}, u32[]{:S(2)}) collective-permute-start(bf16[144,1536]{1,0:T(8,128)(2,1)S(1)} %collective-permute-done.4.refs_3_), channel_id=1, source_target_pairs={{0,1},{1,0},{2,3},{3,2},{4,5},{5,4},{6,7},{7,6},{8,9},{9,8},{10,11... | collective-permute-start | bytes 1327112 | tf_op jit(solution)/shard_map/ppermute | solution.py:27
  69.3 5.1 %collective-permute-start.7 = (bf16[144,1536]{1,0:T(8,128)(2,1)S(1)}, bf16[144,1536]{1,0:T(8,128)(2,1)S(1)}, u32[]{:S(2)}, u32[]{:S(2)}) collective-permute-start(bf16[144,1536]{1,0:T(8,128)(2,1)S(1)} %collective-permute-done.3.refs_2_), channel_id=1, source_target_pairs={{0,1},{1,0},{2,3},{3,2},{4,5},{5,4},{6,7},{7,6},{8,9},{9,8},{10,11... | collective-permute-start | bytes 1327112 | tf_op jit(solution)/shard_map/ppermute | solution.py:27
  70.6 19.2 %collective-permute-start.23 = (bf16[192,1536]{1,0:T(8,128)(2,1)S(1)}, bf16[192,1536]{1,0:T(8,128)(2,1)S(1)}, u32[]{:S(2)}, u32[]{:S(2)}) collective-permute-start(bf16[192,1536]{1,0:T(8,128)(2,1)S(1)} %slice.31), channel_id=1, source_target_pairs={{0,96},{32,0},{64,32},{96,64},{1,97},{33,1},{65,33},{97,65},{2,98}... | collective-permute-start | bytes 1769480 | tf_op jit(solution)/shard_map/ppermute | solution.py:27
  74.4 15.4 %collective-permute-start.21 = (bf16[192,1536]{1,0:T(8,128)(2,1)S(1)}, bf16[192,1536]{1,0:T(8,128)(2,1)S(1)}, u32[]{:S(2)}, u32[]{:S(2)}) collective-permute-start(bf16[192,1536]{1,0:T(8,128)(2,1)S(1)} %slice.30), channel_id=1, source_target_pairs={{0,32},{32,64},{64,96},{96,0},{1,33},{33,65},{65,97},{97,1},{2,34}... | collective-permute-start | bytes 1769480 | tf_op jit(solution)/shard_map/ppermute | solution.py:27
  92.7 15.5 %collective-permute-start.26 = (bf16[192,1536]{1,0:T(8,128)(2,1)S(1)}, bf16[192,1536]{1,0:T(8,128)(2,1)S(1)}, u32[]{:S(2)}, u32[]{:S(2)}) collective-permute-start(bf16[192,1536]{1,0:T(8,128)(2,1)S(1)} %get-tuple-element.69), channel_id=1, source_target_pairs={{0,24},{8,0},{16,8},{24,16},{1,25},{9,1},{17,9},{25,17},{2,26},{10... | collective-permute-start | bytes 1769480 | tf_op jit(solution)/shard_map/ppermute | solution.py:27
  98.7 17.5 %collective-permute-start.14 = (bf16[192,1536]{1,0:T(8,128)(2,1)S(1)}, bf16[192,1536]{1,0:T(8,128)(2,1)S(1)}, u32[]{:S(2)}, u32[]{:S(2)}) collective-permute-start(bf16[192,1536]{1,0:T(8,128)(2,1)S(1)} %get-tuple-element.51), channel_id=1, source_target_pairs={{0,32},{32,64},{64,96},{96,0},{1,33},{33,65},{65,97},{97,1},{2,34}... | collective-permute-start | bytes 1769480 | tf_op jit(solution)/shard_map/ppermute | solution.py:27
  100.4 17.5 %collective-permute-start.18 = (bf16[192,1536]{1,0:T(8,128)(2,1)S(1)}, bf16[192,1536]{1,0:T(8,128)(2,1)S(1)}, u32[]{:S(2)}, u32[]{:S(2)}) collective-permute-start(bf16[192,1536]{1,0:T(8,128)(2,1)S(1)} %get-tuple-element.55), channel_id=1, source_target_pairs={{0,96},{32,0},{64,32},{96,64},{1,97},{33,1},{65,33},{97,65},{2,98}... | collective-permute-start | bytes 1769480 | tf_op jit(solution)/shard_map/ppermute | solution.py:27
  102.6 24.0 %collective-permute-start.16 = (bf16[192,1536]{1,0:T(8,128)(2,1)S(1)}, bf16[192,1536]{1,0:T(8,128)(2,1)S(1)}, u32[]{:S(2)}, u32[]{:S(2)}) collective-permute-start(bf16[192,1536]{1,0:T(8,128)(2,1)S(1)} %get-tuple-element.52), channel_id=1, source_target_pairs={{0,32},{32,64},{64,96},{96,0},{1,33},{33,65},{65,97},{97,1},{2,34}... | collective-permute-start | bytes 1769480 | tf_op jit(solution)/shard_map/ppermute | solution.py:27
  102.6 13.5 %collective-permute-start.24 = (bf16[192,1536]{1,0:T(8,128)(2,1)S(1)}, bf16[192,1536]{1,0:T(8,128)(2,1)S(1)}, u32[]{:S(2)}, u32[]{:S(2)}) collective-permute-start(bf16[192,1536]{1,0:T(8,128)(2,1)S(1)} %get-tuple-element.67), channel_id=1, source_target_pairs={{0,8},{8,16},{16,24},{24,0},{1,9},{9,17},{17,25},{25,1},{2,10},{10... | collective-permute-start | bytes 1769480 | tf_op jit(solution)/shard_map/ppermute | solution.py:27
  108.3 23.8 %collective-permute-start.17 = (bf16[192,1536]{1,0:T(8,128)(2,1)S(1)}, bf16[192,1536]{1,0:T(8,128)(2,1)S(1)}, u32[]{:S(2)}, u32[]{:S(2)}) collective-permute-start(bf16[192,1536]{1,0:T(8,128)(2,1)S(1)} %get-tuple-element.53), channel_id=1, source_target_pairs={{0,96},{32,0},{64,32},{96,64},{1,97},{33,1},{65,33},{97,65},{2,98}... | collective-permute-start | bytes 1769480 | tf_op jit(solution)/shard_map/ppermute | solution.py:27
  116.1 58.5 %collective-permute-start.27 = (bf16[384,1536]{1,0:T(8,128)(2,1)}, bf16[384,1536]{1,0:T(8,128)(2,1)}, u32[]{:S(2)}, u32[]{:S(2)}) collective-permute-start(bf16[384,1536]{1,0:T(8,128)(2,1)} %fusion.1), channel_id=1, source_target_pairs={{0,24},{8,0},{16,8},{24,16},{1,25},{9,1},{17,9},{25,17},{2,26},{10... | collective-permute-start | bytes 3538952 | tf_op jit(solution)/shard_map/ppermute | solution.py:27
  116.3 58.3 %collective-permute-start.25 = (bf16[384,1536]{1,0:T(8,128)(2,1)S(1)}, bf16[384,1536]{1,0:T(8,128)(2,1)}, u32[]{:S(2)}, u32[]{:S(2)}) collective-permute-start(bf16[384,1536]{1,0:T(8,128)(2,1)S(1)} %fusion), channel_id=1, source_target_pairs={{0,8},{8,16},{16,24},{24,0},{1,9},{9,17},{17,25},{25,1},{2,10},{10... | collective-permute-start | bytes 3538952 | tf_op jit(solution)/shard_map/ppermute | solution.py:27
  118.0 21.3 %collective-permute-start.15 = (bf16[192,1536]{1,0:T(8,128)(2,1)S(1)}, bf16[192,1536]{1,0:T(8,128)(2,1)S(1)}, u32[]{:S(2)}, u32[]{:S(2)}) collective-permute-start(bf16[192,1536]{1,0:T(8,128)(2,1)S(1)} %add_convert_fusion.4), channel_id=1, source_target_pairs={{0,32},{32,64},{64,96},{96,0},{1,33},{33,65},{65,97},{97,1},{2,34}... | collective-permute-start | bytes 1769480 | tf_op jit(solution)/shard_map/ppermute | solution.py:27
  126.6 12.6 %collective-permute-start.19 = (bf16[192,1536]{1,0:T(8,128)(2,1)S(1)}, bf16[192,1536]{1,0:T(8,128)(2,1)S(1)}, u32[]{:S(2)}, u32[]{:S(2)}) collective-permute-start(bf16[192,1536]{1,0:T(8,128)(2,1)S(1)} %add_convert_fusion.3), channel_id=1, source_target_pairs={{0,96},{32,0},{64,32},{96,64},{1,97},{33,1},{65,33},{97,65},{2,98}... | collective-permute-start | bytes 1769480 | tf_op jit(solution)/shard_map/ppermute | solution.py:27
  170.5 8.7 %all-to-all-start.1 = ((f32[8,1,384]{2,1,0:T(1,128)}), f32[8,1,384]{2,1,0:T(1,128)S(1)}, u32[]{:S(2)}, u32[]{:S(2)}) async-start(f32[8,1,384]{2,1,0:T(1,128)} %copy-done.1), calls=%async_computation.1 | async-start | bytes 24576 | tf_op jit(solution)/shard_map/all_to_all | solution.py:470
  (3 other events, 8.8 us)

commit v3 on v1

--- a/solution.py
+++ b/solution.py
@@ -273,7 +273,7 @@
             pl.BlockSpec((S, C), lambda i: (0, 0)),
             pl.BlockSpec((128, 128), lambda i: (0, 0)),
         ],
-        out_shape=[pltpu.HBM((S, C), F32), pltpu.HBM((128, 128), F32)],
+        out_shape=[pltpu.HBM((S, C), F32), jax.ShapeDtypeStruct((128, 128), F32)],
         compiler_params=params(24),
         name="fold_grad",
     )(*args)
@@ -338,7 +338,7 @@
         for k in range(count):
             total = jnp.dot(rows[k][0], right, preferred_element_type=F32)
             if own_last:
-                outs[k][:, at] = total
+                outs[k][:, at] = total.astype(BF)
             else:
                 outs[2 * k][:, at] = total[:HALF].astype(BF)
                 outs[2 * k + 1][:, at] = total[HALF:].astype(BF)
@@ -349,7 +349,7 @@
 
 def input_grad(rows, blocks, weights, own):
     half = jax.ShapeDtypeStruct((HALF, C), BF)
-    outs = [pltpu.HBM((S, C), F32)] if own else [half] * (2 * len(blocks))
+    outs = [pltpu.HBM((S, C), BF)] if own else [half] * (2 * len(blocks))
 
     def piece(k):
         return pl.BlockSpec((1, S, C), lambda i: (k, 0, 0))
@@ -443,8 +443,9 @@
     i_near = input_grad(rows, (2, 1), weights, False)
     (i_own,) = input_grad(rows, (0,), weights, True)
     left_a, left_b, right_a, right_b = ring_scatter(i_far, i_near, "x")
-    top = i_own[:HALF] + left_a.astype(F32) + right_a.astype(F32)
-    bottom = i_own[HALF:] + left_b.astype(F32) + right_b.astype(F32)
+    peaks, i_own = lax.optimization_barrier((peaks, i_own))
+    top = i_own[:HALF].astype(F32) + left_a.astype(F32) + right_a.astype(F32)
+    bottom = i_own[HALF:].astype(F32) + left_b.astype(F32) + right_b.astype(F32)
     grad_input = jnp.concatenate([top, bottom], axis=0).astype(BF)
     gradient, pair = fold_grad(parts, CHUNKS, peaks)
     pairs = lax.all_to_all(pair, ALL, 0, 0, tiled=True)

time: 189 us -> 184 us (0.974)
  starting transfers between devices: 62.8 us -> 56.2 us
  waiting for transfers between devices: 76.3 us -> 78.3 us
    all_to_all x1, starting transfers between devices: 13.7 us -> 7.43 us  [step(): pairs = lax.all_to_all(pair, ALL, 0, 0, tiled=True)]
  transfers between devices with their start and end apart: 32 -> 32, of which waited for: 11 -> 12; matrix products, arithmetic and copies ran while one was open for 5% -> 4% of each run, Pallas kernels for 15% -> 15%
where the time goes in v3:
time: 184 us
  waiting for transfers between devices  78.3 us (43%)
  starting transfers between devices  56.2 us (31%)
  Pallas kernels  38.8 us (21%)
  other arithmetic  8.02 us (4%)
    ppermute x30, waiting for transfers between devices, shift(): return lax.ppermute(v, axis, [(i, (i + by) % n) for i in range(n)])  70.5 us
    ppermute x30, starting transfers between devices, shift(): return lax.ppermute(v, axis, [(i, (i + by) % n) for i in range(n)])  44.8 us
    pallas_call x3, Pallas kernels, input_grad(): pl.pallas_call(functools.partial(input_grad_kernel, len(blocks), own), gr...  11.4 us
    pallas_call x1, Pallas kernels, weight_grad(): pl.pallas_call(functools.partial(weight_grad_kernel, blocks, width), grid...  8.42 us
    pallas_call x1, Pallas kernels, adam(): pl.pallas_call(adam_kernel, grid=(S // ROWS,), in_specs=[pl.BlockSpec((12...  8.35 us
    all_to_all x1, starting transfers between devices, step(): pairs = lax.all_to_all(pair, ALL, 0, 0, tiled=True)  7.43 us
    all_to_all x1, waiting for transfers between devices, step(): pairs = lax.all_to_all(pair, ALL, 0, 0, tiled=True)  5.88 us
    all_to_all x1, starting transfers between devices, step(): highs = lax.all_to_all(high, TENSOR, 0, 0, tiled=True)  3.95 us
  transfers between devices with their start and end apart: 32, of which 12 were waited for; matrix products, arithmetic and copies ran while one was open for 4% of the time, Pallas kernels for 15%

profile of v3, /device:TPU:1, one launch (start us, length us, event | category | flops | bytes accessed | tf_op | source)
XLA Modules:
  0.0 183.9 jit_solution(5204289260265618958)
XLA Ops:
  2.0 2.1 %collective-permute-start = (bf16[48,1536]{1,0:T(8,128)(2,1)S(1)}, bf16[48,1536]{1,0:T(8,128)(2,1)S(1)}, u32[]{:S(2)}, u32[]{:S(2)}) collective-permute-start(bf16[48,1536]{1,0:T(8,128)(2,1)S(1)} %get-tuple-element.45), channel_id=1, source_target_pairs={{0,8},{8,16},{16,24},{24,0},{1,9},{9,17},{17,25},{25,1},{2,10},{10... | collective-permute-start | bytes 442376 | tf_op jit(solution)/shard_map/ppermute | solution.py:27
  5.5 2.6 %collective-permute-start.1 = (bf16[48,1536]{1,0:T(8,128)(2,1)S(1)}, bf16[48,1536]{1,0:T(8,128)(2,1)S(1)}, u32[]{:S(2)}, u32[]{:S(2)}) collective-permute-start(bf16[48,1536]{1,0:T(8,128)(2,1)S(1)} %get-tuple-element.46), channel_id=1, source_target_pairs={{0,24},{8,0},{16,8},{24,16},{1,25},{9,1},{17,9},{25,17},{2,26},{10... | collective-permute-start | bytes 442376 | tf_op jit(solution)/shard_map/ppermute | solution.py:27
  8.6 25.2 %collective-permute-done.1 = bf16[48,1536]{1,0:T(8,128)(2,1)S(1)} collective-permute-done((bf16[48,1536]{1,0:T(8,128)(2,1)S(1)}, bf16[48,1536]{1,0:T(8,128)(2,1)S(1)}, u32[]{:S(2)}, u32[]{:S(2)}) %collective-permute-start.1) | collective-permute-done | bytes 147488 | tf_op jit(solution)/shard_map/ppermute | solution.py:27
  33.8 4.4 %collective-permute-done.2 = bf16[48,1536]{1,0:T(8,128)(2,1)S(1)} collective-permute-done((bf16[48,1536]{1,0:T(8,128)(2,1)S(1)}, bf16[48,1536]{1,0:T(8,128)(2,1)S(1)}, u32[]{:S(2)}, u32[]{:S(2)}) %collective-permute-start.2) | collective-permute-done | bytes 147488 | tf_op jit(solution)/shard_map/ppermute | solution.py:27
  39.8 2.9 %collective-permute-start.5 = (bf16[144,1536]{1,0:T(8,128)(2,1)S(1)}, bf16[144,1536]{1,0:T(8,128)(2,1)S(1)}, u32[]{:S(2)}, u32[]{:S(2)}) collective-permute-start(bf16[144,1536]{1,0:T(8,128)(2,1)S(1)} %constant_dynamic-update-slice_fusion.refs_1_), channel_id=1, source_target_pairs={{0,4},{2,6},{4,0},{6,2},{1,5},{3,7},{5,1},{7,3},{8,12},{10,14},{12... | collective-permute-start | bytes 1327112 | tf_op jit(solution)/shard_map/ppermute | solution.py:27
  43.8 3.8 %collective-permute-start.22 = (bf16[384,1536]{1,0:T(8,128)(2,1)S(1)}, bf16[384,1536]{1,0:T(8,128)(2,1)S(1)}, u32[]{:S(2)}, u32[]{:S(2)}) collective-permute-start(bf16[384,1536]{1,0:T(8,128)(2,1)S(1)} %multiply_convert_fusion.refs_5_.refs_6_), channel_id=1, source_target_pairs={{0,96},{32,0},{64,32},{96,64},{1,97},{33,1},{65,33},{97,65},{2,98}... | collective-permute-start | bytes 3538952 | tf_op jit(solution)/shard_map/ppermute | solution.py:27
  47.6 5.3 %collective-permute-done.5.refs_4_ = bf16[144,1536]{1,0:T(8,128)(2,1)S(1)} collective-permute-done((bf16[144,1536]{1,0:T(8,128)(2,1)S(1)}, bf16[144,1536]{1,0:T(8,128)(2,1)S(1)}, u32[]{:S(2)}, u32[]{:S(2)}) %collective-permute-start.5) | collective-permute-done | bytes 442400 | tf_op jit(solution)/shard_map/ppermute | solution.py:27
  54.6 8.2 %collective-permute-done.4.refs_3_ = bf16[144,1536]{1,0:T(8,128)(2,1)S(1)} collective-permute-done((bf16[144,1536]{1,0:T(8,128)(2,1)S(1)}, bf16[144,1536]{1,0:T(8,128)(2,1)S(1)}, u32[]{:S(2)}, u32[]{:S(2)}) %collective-permute-start.4) | collective-permute-done | bytes 442400 | tf_op jit(solution)/shard_map/ppermute | solution.py:27
  65.2 10.0 %collective-permute-done.3.refs_2_ = bf16[144,1536]{1,0:T(8,128)(2,1)S(1)} collective-permute-done((bf16[144,1536]{1,0:T(8,128)(2,1)S(1)}, bf16[144,1536]{1,0:T(8,128)(2,1)S(1)}, u32[]{:S(2)}, u32[]{:S(2)}) %collective-permute-start.3) | collective-permute-done | bytes 442400 | tf_op jit(solution)/shard_map/ppermute | solution.py:27
  76.9 2.0 %collective-permute-start.7 = (bf16[144,1536]{1,0:T(8,128)(2,1)S(1)}, bf16[144,1536]{1,0:T(8,128)(2,1)S(1)}, u32[]{:S(2)}, u32[]{:S(2)}) collective-permute-start(bf16[144,1536]{1,0:T(8,128)(2,1)S(1)} %collective-permute-done.3.refs_2_), channel_id=1, source_target_pairs={{0,1},{1,0},{2,3},{3,2},{4,5},{5,4},{6,7},{7,6},{8,9},{9,8},{10,11... | collective-permute-start | bytes 1327112 | tf_op jit(solution)/shard_map/ppermute | solution.py:27
  82.0 3.8 %collective-permute-start.23 = (bf16[192,1536]{1,0:T(8,128)(2,1)S(1)}, bf16[192,1536]{1,0:T(8,128)(2,1)S(1)}, u32[]{:S(2)}, u32[]{:S(2)}) collective-permute-start(bf16[192,1536]{1,0:T(8,128)(2,1)S(1)} %slice.31), channel_id=1, source_target_pairs={{0,96},{32,0},{64,32},{96,64},{1,97},{33,1},{65,33},{97,65},{2,98}... | collective-permute-start | bytes 1769480 | tf_op jit(solution)/shard_map/ppermute | solution.py:27
  85.9 2.8 %far_start.1 = (f32[384,1536]{1,0:T(8,128)S(1)}, f32[8,256]{1,0:T(8,128)S(1)}) custom-call(bf16[4,384,1536]{2,1,0:T(8,128)(2,1)S(1)} %get-tuple-element.48.refs_0_.refs_1_.refs_2_.cols_ref, bf16[384,1536]{1,0:T(8,128)(2,1)S(1)} %copy-done.1, bf16[384,1536]{1,0:T(8,128)(2,1)S(1)} %collective-permute-done.10.refs_4_.left_ref, ...), custom_call_target="tpu_custom_call" | custom-call | flops 1358954496 | bytes 6291456 | tf_op jit(solution)/shard_map/far_start/pallas_call | solution.py:200
  88.8 2.2 %collective-permute-done.12.refs_6_.top_ref = bf16[192,1536]{1,0:T(8,128)(2,1)S(1)} collective-permute-done((bf16[192,1536]{1,0:T(8,128)(2,1)S(1)}, bf16[192,1536]{1,0:T(8,128)(2,1)S(1)}, u32[]{:S(2)}, u32[]{:S(2)}) %collective-permute-start.12) | collective-permute-done | bytes 589856 | tf_op jit(solution)/shard_map/ppermute | solution.py:27
  94.3 8.4 %weight_grad.1 = (bf16[192,1536]{1,0:T(8,128)(2,1)S(1)}, bf16[192,1536]{1,0:T(8,128)(2,1)S(1)}, bf16[192,1536]{1,0:T(8,128)(2,1)S(1)}, bf16[192,1536]{1,0:T(8,12...) custom-call(bf16[4,384,1536]{2,1,0:T(8,128)(2,1)S(1)} %get-tuple-element.48.refs_0_.refs_1_.refs_2_.cols_ref, ...), custom_call_target="tpu_custom_call" | custom-call | flops 5435817984 | bytes 9437184 | tf_op jit(solution)/shard_map/weight_grad/pallas_call | solution.py:143
  102.8 2.2 %collective-permute-start.18 = (bf16[192,1536]{1,0:T(8,128)(2,1)S(1)}, bf16[192,1536]{1,0:T(8,128)(2,1)S(1)}, u32[]{:S(2)}, u32[]{:S(2)}) collective-permute-start(bf16[192,1536]{1,0:T(8,128)(2,1)S(1)} %get-tuple-element.57), channel_id=1, source_target_pairs={{0,96},{32,0},{64,32},{96,64},{1,97},{33,1},{65,33},{97,65},{2,98}... | collective-permute-start | bytes 1769480 | tf_op jit(solution)/shard_map/ppermute | solution.py:27
  105.0 2.7 %collective-permute-start.17 = (bf16[192,1536]{1,0:T(8,128)(2,1)S(1)}, bf16[192,1536]{1,0:T(8,128)(2,1)S(1)}, u32[]{:S(2)}, u32[]{:S(2)}) collective-permute-start(bf16[192,1536]{1,0:T(8,128)(2,1)S(1)} %get-tuple-element.55), channel_id=1, source_target_pairs={{0,96},{32,0},{64,32},{96,64},{1,97},{33,1},{65,33},{97,65},{2,98}... | collective-permute-start | bytes 1769480 | tf_op jit(solution)/shard_map/ppermute | solution.py:27
  107.6 2.9 %input_grad.5 = (bf16[192,1536]{1,0:T(8,128)(2,1)S(1)}, bf16[192,1536]{1,0:T(8,128)(2,1)S(1)}) custom-call(bf16[4,384,1536]{2,1,0:T(8,128)(2,1)S(1)} %get-tuple-element.61.refs_0_.refs_1_, bf16[192,1536]{1,0:T(8,128)(2,1)S(1)} %collective-permute-done.21.refs_1_.refs_2_, bf16[192,1536]{1,0:T(8,128)(2,1)S(1)} %collective-permute-done.23.refs_2_.refs_3_, ...), custom_call_target="tpu_custom_call" | custom-call | flops 1811939328 | bytes 9437184 | tf_op jit(solution)/shard_map/input_grad/pallas_call | solution.py:360
  110.8 4.7 %input_grad.4 = (bf16[192,1536]{1,0:T(8,128)(2,1)S(1)}, bf16[192,1536]{1,0:T(8,128)(2,1)S(1)}, bf16[192,1536]{1,0:T(8,128)(2,1)S(1)}, bf16[192,1536]{1,0:T(8,128)(2,1)S(1)}) custom-call(bf16[4,384,1536]{2,1,0:T(8,128)(2,1)S(1)} %get-tuple-element.61.refs_0_.refs_1_, bf16[4,384,1536]{2,1,0:T(8,128)(2,1)S(1)} %get-tuple-element.61.refs_0_.refs_1_, ...), custom_call_target="tpu_custom_call" | custom-call | flops 3623878656 | bytes 9437184 | tf_op jit(solution)/shard_map/input_grad/pallas_call | solution.py:360
  115.5 2.7 %collective-permute-start.28 = (bf16[192,1536]{1,0:T(8,128)(2,1)S(1)}, bf16[192,1536]{1,0:T(8,128)(2,1)S(1)}, u32[]{:S(2)}, u32[]{:S(2)}) collective-permute-start(bf16[192,1536]{1,0:T(8,128)(2,1)S(1)} %get-tuple-element.73), channel_id=1, source_target_pairs={{0,24},{8,0},{16,8},{24,16},{1,25},{9,1},{17,9},{25,17},{2,26},{10... | collective-permute-start | bytes 1769480 | tf_op jit(solution)/shard_map/ppermute | solution.py:27
  118.6 4.7 %collective-permute-done.24 = bf16[192,1536]{1,0:T(8,128)(2,1)S(1)} collective-permute-done((bf16[192,1536]{1,0:T(8,128)(2,1)S(1)}, bf16[192,1536]{1,0:T(8,128)(2,1)S(1)}, u32[]{:S(2)}, u32[]{:S(2)}) %collective-permute-start.24) | collective-permute-done | bytes 589856 | tf_op jit(solution)/shard_map/ppermute | solution.py:27
  124.2 2.8 %collective-permute-done.28 = bf16[192,1536]{1,0:T(8,128)(2,1)S(1)} collective-permute-done((bf16[192,1536]{1,0:T(8,128)(2,1)S(1)}, bf16[192,1536]{1,0:T(8,128)(2,1)S(1)}, u32[]{:S(2)}, u32[]{:S(2)}) %collective-permute-start.28) | collective-permute-done | bytes 589856 | tf_op jit(solution)/shard_map/ppermute | solution.py:27
  129.8 6.2 %collective-permute-done.15.refs_1_ = bf16[192,1536]{1,0:T(8,128)(2,1)S(1)} collective-permute-done((bf16[192,1536]{1,0:T(8,128)(2,1)S(1)}, bf16[192,1536]{1,0:T(8,128)(2,1)S(1)}, u32[]{:S(2)}, u32[]{:S(2)}) %collective-permute-start.15) | collective-permute-done | bytes 589856 | tf_op jit(solution)/shard_map/ppermute | solution.py:27
  136.0 6.1 %collective-permute-start.29 = (bf16[192,1536]{1,0:T(8,128)(2,1)}, bf16[192,1536]{1,0:T(8,128)(2,1)}, u32[]{:S(2)}, u32[]{:S(2)}) collective-permute-start(bf16[192,1536]{1,0:T(8,128)(2,1)} %add_convert_fusion.1), channel_id=1, source_target_pairs={{0,24},{8,0},{16,8},{24,16},{1,25},{9,1},{17,9},{25,17},{2,26},{10... | collective-permute-start | bytes 1769480 | tf_op jit(solution)/shard_map/ppermute | solution.py:27
  142.2 3.9 %input_grad.3 = bf16[384,1536]{1,0:T(8,128)(2,1)} custom-call(bf16[4,384,1536]{2,1,0:T(8,128)(2,1)S(1)} %get-tuple-element.61.refs_0_.refs_1_, bf16[192,1536]{1,0:T(8,128)(2,1)S(1)} %collective-permute-done.21.refs_1_.refs_2_, bf16[192,1536]{1,0:T(8,128)(2,1)S(1)} %collective-permute-done.23.refs_2_.refs_3_, ...), custom_call_target="tpu_custom_call" | custom-call | flops 1811939328 | bytes 9437184 | tf_op jit(solution)/shard_map/input_grad/pallas_call | solution.py:360
  146.1 2.0 %fold_grad.1 = (f32[384,1536]{1,0:T(8,128)}, f32[128,128]{1,0:T(8,128)}) custom-call(f32[384,1536]{1,0:T(8,128)S(1)} %get-tuple-element.49.refs_0_, bf16[192,1536]{1,0:T(8,128)(2,1)S(1)} %collective-permute-done.15.refs_1_, bf16[192,1536]{1,0:T(8,128)(2,1)S(1)} %collective-permute-done.16.refs_2_, bf16[192,1536]{1,0:T(8,128)(2,1)S(1)} %collective-permute-done.17.refs_3_, ...), custom_call_target="tpu_custom_call" | custom-call | tf_op jit(solution)/shard_map/fold_grad/pallas_call | solution.py:268
  148.1 7.4 %all-to-all-start = ((f32[128,1,128]{2,1,0:T(1,128)}), f32[128,1,128]{2,1,0:T(1,128)S(1)}, u32[]{:S(2)}, u32[]{:S(2)}) async-start(f32[128,1,128]{2,1,0:T(1,128)} %bitcast.1), calls=%async_computation | async-start | bytes 131072 | tf_op jit(solution)/shard_map/all_to_all | solution.py:451
  156.3 2.8 %add_convert_fusion.2 = (bf16[192,1536]{1,0:T(8,128)(2,1)S(1)}, bf16[192,1536]{1,0:T(8,128)(2,1)}) fusion(bf16[192,1536]{1,0:T(8,128)(2,1)} %copy-done.4, bf16[192,1536]{1,0:T(8,128)(2,1)} %collective-permute-done.25, bf16[384,1536]{1,0:T(8,128)(2,1)S(1)} %copy-done.2, bf16[192,1536]{1,0:T(8,128)(2,1)} %collective-permute-done.29, ...), kind=kLoop, calls=%fused_computation.4 | loop fusion | flops 3538944 | bytes 4718592 | tf_op jit(solution)/shard_map/convert
  159.2 5.9 %all-to-all-done = f32[128,1,128]{2,1,0:T(1,128)S(1)} async-done(((f32[128,1,128]{2,1,0:T(1,128)}), f32[128,1,128]{2,1,0:T(1,128)S(1)}, u32[]{:S(2)}, u32[]{:S(2)}) %all-to-all-start) | async-done | bytes 65568 | tf_op jit(solution)/shard_map/all_to_all | solution.py:451
  165.1 8.3 %adam.1 = (f32[384,1536]{1,0:T(8,128)}, f32[384,1536]{1,0:T(8,128)}, f32[384,1536]{1,0:T(8,128)}, f32[8,1,384]{2,1,0:T(1,128)}, f32[8,128]{1,0:T(8,128)S(1)}, /*index=5*/f32[384,1536]{1,0:T(8,128)S(1)}) custom-call(f32[128,128]{1,0:T(8,128)S(1)} %bitcast.5, f32[384,1536]{1,0:T(8,128)} %get-tuple-element.65.grad_ref, f32[384,1536]{1,0:T(8,128)} %moment_ref.1, ...), custom_call_target="tpu_custom_call" | custom-call | tf_op jit(solution)/shard_map/adam/pallas_call | solution.py:318
  173.4 4.0 %all-to-all-start.1 = ((f32[8,1,384]{2,1,0:T(1,128)}), f32[8,1,384]{2,1,0:T(1,128)S(1)}, u32[]{:S(2)}, u32[]{:S(2)}) async-start(f32[8,1,384]{2,1,0:T(1,128)} %get-tuple-element.66), calls=%async_computation.1 | async-start | bytes 24576 | tf_op jit(solution)/shard_map/all_to_all | solution.py:459
  177.4 2.2 %pad_maximum_fusion = bf16[384,1536]{1,0:T(8,128)(2,1)} fusion(bf16[192,1536]{1,0:T(8,128)(2,1)} %get-tuple-element.84, bf16[192,1536]{1,0:T(8,128)(2,1)S(1)} %get-tuple-element.83), kind=kLoop, calls=%fused_computation.1 | loop fusion | flops 2359296 | bytes 2359296 | tf_op jit(solution)/shard_map/concatenate | solution.py:449
  180.1 1.9 %all-to-all-done.1.highs_ref = f32[8,1,384]{2,1,0:T(1,128)S(1)} async-done(((f32[8,1,384]{2,1,0:T(1,128)}), f32[8,1,384]{2,1,0:T(1,128)S(1)}, u32[]{:S(2)}, u32[]{:S(2)}) %all-to-all-start.1) | async-done | bytes 12320 | tf_op jit(solution)/shard_map/all_to_all | solution.py:459
  (72 shorter events, 25.7 us)
Async XLA Ops:
  2.0 6.6 %collective-permute-start = (bf16[48,1536]{1,0:T(8,128)(2,1)S(1)}, bf16[48,1536]{1,0:T(8,128)(2,1)S(1)}, u32[]{:S(2)}, u32[]{:S(2)}) collective-permute-start(bf16[48,1536]{1,0:T(8,128)(2,1)S(1)} %get-tuple-element.45), channel_id=1, source_target_pairs={{0,8},{8,16},{16,24},{24,0},{1,9},{9,17},{17,25},{25,1},{2,10},{10... | collective-permute-start | bytes 442376 | tf_op jit(solution)/shard_map/ppermute | solution.py:27
  4.1 60.2 %collective-permute-start.11 = (bf16[384,1536]{1,0:T(8,128)(2,1)S(1)}, bf16[384,1536]{1,0:T(8,128)(2,1)S(1)}, u32[]{:S(2)}, u32[]{:S(2)}) collective-permute-start(bf16[384,1536]{1,0:T(8,128)(2,1)S(1)} %copy-done.1), channel_id=1, source_target_pairs={{0,24},{8,0},{16,8},{24,16},{1,25},{9,1},{17,9},{25,17},{2,26},{10... | collective-permute-start | bytes 3538952 | tf_op jit(solution)/shard_map/ppermute | solution.py:27
  5.4 59.6 %collective-permute-start.10 = (bf16[384,1536]{1,0:T(8,128)(2,1)S(1)}, bf16[384,1536]{1,0:T(8,128)(2,1)S(1)}, u32[]{:S(2)}, u32[]{:S(2)}) collective-permute-start(bf16[384,1536]{1,0:T(8,128)(2,1)S(1)} %copy-done.1), channel_id=1, source_target_pairs={{0,8},{8,16},{16,24},{24,0},{1,9},{9,17},{17,25},{25,1},{2,10},{10... | collective-permute-start | bytes 3538952 | tf_op jit(solution)/shard_map/ppermute | solution.py:27
  5.5 28.3 %collective-permute-start.1 = (bf16[48,1536]{1,0:T(8,128)(2,1)S(1)}, bf16[48,1536]{1,0:T(8,128)(2,1)S(1)}, u32[]{:S(2)}, u32[]{:S(2)}) collective-permute-start(bf16[48,1536]{1,0:T(8,128)(2,1)S(1)} %get-tuple-element.46), channel_id=1, source_target_pairs={{0,24},{8,0},{16,8},{24,16},{1,25},{9,1},{17,9},{25,17},{2,26},{10... | collective-permute-start | bytes 442376 | tf_op jit(solution)/shard_map/ppermute | solution.py:27
  8.1 30.1 %collective-permute-start.2 = (bf16[48,1536]{1,0:T(8,128)(2,1)S(1)}, bf16[48,1536]{1,0:T(8,128)(2,1)S(1)}, u32[]{:S(2)}, u32[]{:S(2)}) collective-permute-start(bf16[48,1536]{1,0:T(8,128)(2,1)S(1)} %get-tuple-element.47), channel_id=1, source_target_pairs={{0,16},{8,24},{16,0},{24,8},{1,17},{9,25},{17,1},{25,9},{2,18},{10... | collective-permute-start | bytes 442376 | tf_op jit(solution)/shard_map/ppermute | solution.py:27
  38.2 5.6 %collective-permute-start.6 = (bf16[144,1536]{1,0:T(8,128)(2,1)S(1)}, bf16[144,1536]{1,0:T(8,128)(2,1)S(1)}, u32[]{:S(2)}, u32[]{:S(2)}) collective-permute-start(bf16[144,1536]{1,0:T(8,128)(2,1)S(1)} %constant_dynamic-update-slice_fusion.refs_1_), channel_id=1, source_target_pairs={{0,1},{1,0},{2,3},{3,2},{4,5},{5,4},{6,7},{7,6},{8,9},{9,8},{10,11... | collective-permute-start | bytes 1327112 | tf_op jit(solution)/shard_map/ppermute | solution.py:27
  39.8 13.1 %collective-permute-start.5 = (bf16[144,1536]{1,0:T(8,128)(2,1)S(1)}, bf16[144,1536]{1,0:T(8,128)(2,1)S(1)}, u32[]{:S(2)}, u32[]{:S(2)}) collective-permute-start(bf16[144,1536]{1,0:T(8,128)(2,1)S(1)} %constant_dynamic-update-slice_fusion.refs_1_), channel_id=1, source_target_pairs={{0,4},{2,6},{4,0},{6,2},{1,5},{3,7},{5,1},{7,3},{8,12},{10,14},{12... | collective-permute-start | bytes 1327112 | tf_op jit(solution)/shard_map/ppermute | solution.py:27
  42.8 20.1 %collective-permute-start.4 = (bf16[144,1536]{1,0:T(8,128)(2,1)S(1)}, bf16[144,1536]{1,0:T(8,128)(2,1)S(1)}, u32[]{:S(2)}, u32[]{:S(2)}) collective-permute-start(bf16[144,1536]{1,0:T(8,128)(2,1)S(1)} %constant_dynamic-update-slice_fusion.refs_1_), channel_id=1, source_target_pairs={{0,6},{2,0},{4,2},{6,4},{1,7},{3,1},{5,3},{7,5},{8,14},{10,8},{12,... | collective-permute-start | bytes 1327112 | tf_op jit(solution)/shard_map/ppermute | solution.py:27
  43.8 38.1 %collective-permute-start.22 = (bf16[384,1536]{1,0:T(8,128)(2,1)S(1)}, bf16[384,1536]{1,0:T(8,128)(2,1)S(1)}, u32[]{:S(2)}, u32[]{:S(2)}) collective-permute-start(bf16[384,1536]{1,0:T(8,128)(2,1)S(1)} %multiply_convert_fusion.refs_5_.refs_6_), channel_id=1, source_target_pairs={{0,96},{32,0},{64,32},{96,64},{1,97},{33,1},{65,33},{97,65},{2,98}... | collective-permute-start | bytes 3538952 | tf_op jit(solution)/shard_map/ppermute | solution.py:27
  53.0 32.8 %collective-permute-start.20 = (bf16[384,1536]{1,0:T(8,128)(2,1)S(1)}, bf16[384,1536]{1,0:T(8,128)(2,1)S(1)}, u32[]{:S(2)}, u32[]{:S(2)}) collective-permute-start(bf16[384,1536]{1,0:T(8,128)(2,1)S(1)} %multiply_convert_fusion.refs_5_.refs_6_), channel_id=1, source_target_pairs={{0,32},{32,64},{64,96},{96,0},{1,33},{33,65},{65,97},{97,1},{2,34}... | collective-permute-start | bytes 3538952 | tf_op jit(solution)/shard_map/ppermute | solution.py:27
  62.8 12.3 %collective-permute-start.3 = (bf16[144,1536]{1,0:T(8,128)(2,1)S(1)}, bf16[144,1536]{1,0:T(8,128)(2,1)S(1)}, u32[]{:S(2)}, u32[]{:S(2)}) collective-permute-start(bf16[144,1536]{1,0:T(8,128)(2,1)S(1)} %constant_dynamic-update-slice_fusion.refs_1_), channel_id=1, source_target_pairs={{0,2},{2,4},{4,6},{6,0},{1,3},{3,5},{5,7},{7,1},{8,10},{10,12},{12... | collective-permute-start | bytes 1327112 | tf_op jit(solution)/shard_map/ppermute | solution.py:27
  64.2 12.6 %collective-permute-start.9 = (bf16[144,1536]{1,0:T(8,128)(2,1)S(1)}, bf16[144,1536]{1,0:T(8,128)(2,1)S(1)}, u32[]{:S(2)}, u32[]{:S(2)}) collective-permute-start(bf16[144,1536]{1,0:T(8,128)(2,1)S(1)} %collective-permute-done.5.refs_4_), channel_id=1, source_target_pairs={{0,1},{1,0},{2,3},{3,2},{4,5},{5,4},{6,7},{7,6},{8,9},{9,8},{10,11... | collective-permute-start | bytes 1327112 | tf_op jit(solution)/shard_map/ppermute | solution.py:27
  65.0 11.9 %collective-permute-start.8 = (bf16[144,1536]{1,0:T(8,128)(2,1)S(1)}, bf16[144,1536]{1,0:T(8,128)(2,1)S(1)}, u32[]{:S(2)}, u32[]{:S(2)}) collective-permute-start(bf16[144,1536]{1,0:T(8,128)(2,1)S(1)} %collective-permute-done.4.refs_3_), channel_id=1, source_target_pairs={{0,1},{1,0},{2,3},{3,2},{4,5},{5,4},{6,7},{7,6},{8,9},{9,8},{10,11... | collective-permute-start | bytes 1327112 | tf_op jit(solution)/shard_map/ppermute | solution.py:27
  75.1 13.7 %collective-permute-start.13 = (bf16[192,1536]{1,0:T(8,128)(2,1)S(1)}, bf16[192,1536]{1,0:T(8,128)(2,1)S(1)}, u32[]{:S(2)}, u32[]{:S(2)}) collective-permute-start(bf16[192,1536]{1,0:T(8,128)(2,1)S(1)} %slice.29), channel_id=1, source_target_pairs={{0,24},{8,0},{16,8},{24,16},{1,25},{9,1},{17,9},{25,17},{2,26},{10... | collective-permute-start | bytes 1769480 | tf_op jit(solution)/shard_map/ppermute | solution.py:27
  76.9 14.2 %collective-permute-start.12 = (bf16[192,1536]{1,0:T(8,128)(2,1)S(1)}, bf16[192,1536]{1,0:T(8,128)(2,1)S(1)}, u32[]{:S(2)}, u32[]{:S(2)}) collective-permute-start(bf16[192,1536]{1,0:T(8,128)(2,1)S(1)} %slice.28), channel_id=1, source_target_pairs={{0,8},{8,16},{16,24},{24,0},{1,9},{9,17},{17,25},{25,1},{2,10},{10... | collective-permute-start | bytes 1769480 | tf_op jit(solution)/shard_map/ppermute | solution.py:27
  76.9 3.4 %collective-permute-start.7 = (bf16[144,1536]{1,0:T(8,128)(2,1)S(1)}, bf16[144,1536]{1,0:T(8,128)(2,1)S(1)}, u32[]{:S(2)}, u32[]{:S(2)}) collective-permute-start(bf16[144,1536]{1,0:T(8,128)(2,1)S(1)} %collective-permute-done.3.refs_2_), channel_id=1, source_target_pairs={{0,1},{1,0},{2,3},{3,2},{4,5},{5,4},{6,7},{7,6},{8,9},{9,8},{10,11... | collective-permute-start | bytes 1327112 | tf_op jit(solution)/shard_map/ppermute | solution.py:27
  82.0 23.0 %collective-permute-start.23 = (bf16[192,1536]{1,0:T(8,128)(2,1)S(1)}, bf16[192,1536]{1,0:T(8,128)(2,1)S(1)}, u32[]{:S(2)}, u32[]{:S(2)}) collective-permute-start(bf16[192,1536]{1,0:T(8,128)(2,1)S(1)} %slice.31), channel_id=1, source_target_pairs={{0,96},{32,0},{64,32},{96,64},{1,97},{33,1},{65,33},{97,65},{2,98}... | collective-permute-start | bytes 1769480 | tf_op jit(solution)/shard_map/ppermute | solution.py:27
  85.8 21.8 %collective-permute-start.21 = (bf16[192,1536]{1,0:T(8,128)(2,1)S(1)}, bf16[192,1536]{1,0:T(8,128)(2,1)S(1)}, u32[]{:S(2)}, u32[]{:S(2)}) collective-permute-start(bf16[192,1536]{1,0:T(8,128)(2,1)S(1)} %slice.30), channel_id=1, source_target_pairs={{0,32},{32,64},{64,96},{96,0},{1,33},{33,65},{65,97},{97,1},{2,34}... | collective-permute-start | bytes 1769480 | tf_op jit(solution)/shard_map/ppermute | solution.py:27
  92.6 22.8 %collective-permute-start.14 = (bf16[192,1536]{1,0:T(8,128)(2,1)S(1)}, bf16[192,1536]{1,0:T(8,128)(2,1)S(1)}, u32[]{:S(2)}, u32[]{:S(2)}) collective-permute-start(bf16[192,1536]{1,0:T(8,128)(2,1)S(1)} %get-tuple-element.53), channel_id=1, source_target_pairs={{0,32},{32,64},{64,96},{96,0},{1,33},{33,65},{65,97},{97,1},{2,34}... | collective-permute-start | bytes 1769480 | tf_op jit(solution)/shard_map/ppermute | solution.py:27
  102.8 15.6 %collective-permute-start.18 = (bf16[192,1536]{1,0:T(8,128)(2,1)S(1)}, bf16[192,1536]{1,0:T(8,128)(2,1)S(1)}, u32[]{:S(2)}, u32[]{:S(2)}) collective-permute-start(bf16[192,1536]{1,0:T(8,128)(2,1)S(1)} %get-tuple-element.57), channel_id=1, source_target_pairs={{0,96},{32,0},{64,32},{96,64},{1,97},{33,1},{65,33},{97,65},{2,98}... | collective-permute-start | bytes 1769480 | tf_op jit(solution)/shard_map/ppermute | solution.py:27
  105.0 23.0 %collective-permute-start.16 = (bf16[192,1536]{1,0:T(8,128)(2,1)S(1)}, bf16[192,1536]{1,0:T(8,128)(2,1)S(1)}, u32[]{:S(2)}, u32[]{:S(2)}) collective-permute-start(bf16[192,1536]{1,0:T(8,128)(2,1)S(1)} %get-tuple-element.54), channel_id=1, source_target_pairs={{0,32},{32,64},{64,96},{96,0},{1,33},{33,65},{65,97},{97,1},{2,34}... | collective-permute-start | bytes 1769480 | tf_op jit(solution)/shard_map/ppermute | solution.py:27
  105.0 23.0 %collective-permute-start.17 = (bf16[192,1536]{1,0:T(8,128)(2,1)S(1)}, bf16[192,1536]{1,0:T(8,128)(2,1)S(1)}, u32[]{:S(2)}, u32[]{:S(2)}) collective-permute-start(bf16[192,1536]{1,0:T(8,128)(2,1)S(1)} %get-tuple-element.55), channel_id=1, source_target_pairs={{0,96},{32,0},{64,32},{96,64},{1,97},{33,1},{65,33},{97,65},{2,98}... | collective-permute-start | bytes 1769480 | tf_op jit(solution)/shard_map/ppermute | solution.py:27
  110.5 12.7 %collective-permute-start.24 = (bf16[192,1536]{1,0:T(8,128)(2,1)S(1)}, bf16[192,1536]{1,0:T(8,128)(2,1)S(1)}, u32[]{:S(2)}, u32[]{:S(2)}) collective-permute-start(bf16[192,1536]{1,0:T(8,128)(2,1)S(1)} %get-tuple-element.69), channel_id=1, source_target_pairs={{0,8},{8,16},{16,24},{24,0},{1,9},{9,17},{17,25},{25,1},{2,10},{10... | collective-permute-start | bytes 1769480 | tf_op jit(solution)/shard_map/ppermute | solution.py:27
  115.5 11.5 %collective-permute-start.28 = (bf16[192,1536]{1,0:T(8,128)(2,1)S(1)}, bf16[192,1536]{1,0:T(8,128)(2,1)S(1)}, u32[]{:S(2)}, u32[]{:S(2)}) collective-permute-start(bf16[192,1536]{1,0:T(8,128)(2,1)S(1)} %get-tuple-element.73), channel_id=1, source_target_pairs={{0,24},{8,0},{16,8},{24,16},{1,25},{9,1},{17,9},{25,17},{2,26},{10... | collective-permute-start | bytes 1769480 | tf_op jit(solution)/shard_map/ppermute | solution.py:27
  118.3 37.2 %collective-permute-start.26 = (bf16[192,1536]{1,0:T(8,128)(2,1)S(1)}, bf16[192,1536]{1,0:T(8,128)(2,1)S(1)}, u32[]{:S(2)}, u32[]{:S(2)}) collective-permute-start(bf16[192,1536]{1,0:T(8,128)(2,1)S(1)} %get-tuple-element.70), channel_id=1, source_target_pairs={{0,24},{8,0},{16,8},{24,16},{1,25},{9,1},{17,9},{25,17},{2,26},{10... | collective-permute-start | bytes 1769480 | tf_op jit(solution)/shard_map/ppermute | solution.py:27
  123.2 12.8 %collective-permute-start.15 = (bf16[192,1536]{1,0:T(8,128)(2,1)S(1)}, bf16[192,1536]{1,0:T(8,128)(2,1)S(1)}, u32[]{:S(2)}, u32[]{:S(2)}) collective-permute-start(bf16[192,1536]{1,0:T(8,128)(2,1)S(1)} %add_convert_fusion.5), channel_id=1, source_target_pairs={{0,32},{32,64},{64,96},{96,0},{1,33},{33,65},{65,97},{97,1},{2,34}... | collective-permute-start | bytes 1769480 | tf_op jit(solution)/shard_map/ppermute | solution.py:27
  127.0 19.1 %collective-permute-start.19 = (bf16[192,1536]{1,0:T(8,128)(2,1)S(1)}, bf16[192,1536]{1,0:T(8,128)(2,1)S(1)}, u32[]{:S(2)}, u32[]{:S(2)}) collective-permute-start(bf16[192,1536]{1,0:T(8,128)(2,1)S(1)} %add_convert_fusion.4), channel_id=1, source_target_pairs={{0,96},{32,0},{64,32},{96,64},{1,97},{33,1},{65,33},{97,65},{2,98}... | collective-permute-start | bytes 1769480 | tf_op jit(solution)/shard_map/ppermute | solution.py:27
  127.9 27.6 %collective-permute-start.27 = (bf16[192,1536]{1,0:T(8,128)(2,1)S(1)}, bf16[192,1536]{1,0:T(8,128)(2,1)}, u32[]{:S(2)}, u32[]{:S(2)}) collective-permute-start(bf16[192,1536]{1,0:T(8,128)(2,1)S(1)} %get-tuple-element.71), channel_id=1, source_target_pairs={{0,8},{8,16},{16,24},{24,0},{1,9},{9,17},{17,25},{25,1},{2,10},{10... | collective-permute-start | bytes 1769480 | tf_op jit(solution)/shard_map/ppermute | solution.py:27
  127.9 27.6 %collective-permute-start.25 = (bf16[192,1536]{1,0:T(8,128)(2,1)}, bf16[192,1536]{1,0:T(8,128)(2,1)}, u32[]{:S(2)}, u32[]{:S(2)}) collective-permute-start(bf16[192,1536]{1,0:T(8,128)(2,1)} %add_convert_fusion.3), channel_id=1, source_target_pairs={{0,8},{8,16},{16,24},{24,0},{1,9},{9,17},{17,25},{25,1},{2,10},{10... | collective-permute-start | bytes 1769480 | tf_op jit(solution)/shard_map/ppermute | solution.py:27
  136.0 20.3 %collective-permute-start.29 = (bf16[192,1536]{1,0:T(8,128)(2,1)}, bf16[192,1536]{1,0:T(8,128)(2,1)}, u32[]{:S(2)}, u32[]{:S(2)}) collective-permute-start(bf16[192,1536]{1,0:T(8,128)(2,1)} %add_convert_fusion.1), channel_id=1, source_target_pairs={{0,24},{8,0},{16,8},{24,16},{1,25},{9,1},{17,9},{25,17},{2,26},{10... | collective-permute-start | bytes 1769480 | tf_op jit(solution)/shard_map/ppermute | solution.py:27
  148.1 17.0 %all-to-all-start = ((f32[128,1,128]{2,1,0:T(1,128)}), f32[128,1,128]{2,1,0:T(1,128)S(1)}, u32[]{:S(2)}, u32[]{:S(2)}) async-start(f32[128,1,128]{2,1,0:T(1,128)} %bitcast.1), calls=%async_computation | async-start | bytes 131072 | tf_op jit(solution)/shard_map/all_to_all | solution.py:451
  173.4 8.6 %all-to-all-start.1 = ((f32[8,1,384]{2,1,0:T(1,128)}), f32[8,1,384]{2,1,0:T(1,128)S(1)}, u32[]{:S(2)}, u32[]{:S(2)}) async-start(f32[8,1,384]{2,1,0:T(1,128)} %get-tuple-element.66), calls=%async_computation.1 | async-start | bytes 24576 | tf_op jit(solution)/shard_map/all_to_all | solution.py:459
  (6 other events, 102.1 us)
